TPU v7x, 32 devices: a whole 2x2x4 slice. The times are simulated.
32 devices in a mesh: nodes: 16 (over z, y, x), fsdp: 2 (over core).
Axes of the slice: x: 2, y: 2, z: 4, core: 2. Of those that a mesh axis runs over, the one named last changes fastest.
Arguments:
- features: bfloat16 [49152, 512], P(('nodes', 'fsdp')), may hold values from -6 to 6
- targets: float32 [49152], P(('nodes', 'fsdp')), may hold values from -6 to 6
- node_mask: int32 [49152], P(('nodes', 'fsdp')), may hold values 0 or 1
- block_counts: int32 [32], P(('nodes', 'fsdp')), may hold values from 1 to 12, as said below
- neighbours: int32 [384, 8], P(('nodes', 'fsdp')), may hold values from 0 to 11, as said below
- edge_types: int32 [384, 9], P(('nodes', 'fsdp')), may hold values from 0 to 63
- proj_weights: float32 [5, 512, 512], P(None, ('nodes', 'fsdp'))
- ffn_weights: float32 [2, 512, 2048], P(None, ('nodes', 'fsdp'))
- vector_params: float32 [8, 512], P(None, ('nodes', 'fsdp'))
- proj_mean: float32 [5, 512, 512], P(None, ('nodes', 'fsdp')), may hold values from -0.009765625 to 0.009765625
- ffn_mean: float32 [2, 512, 2048], P(None, ('nodes', 'fsdp')), may hold values from -0.009765625 to 0.009765625
- vector_mean: float32 [8, 512], P(None, ('nodes', 'fsdp')), may hold values from -0.009765625 to 0.009765625
- proj_square: float32 [5, 512, 512], P(None, ('nodes', 'fsdp')), may hold values from 1.0172526e-08 to 1.0172526e-07
- ffn_square: float32 [2, 512, 2048], P(None, ('nodes', 'fsdp')), may hold values from 1.0172526e-08 to 1.0172526e-07
- vector_square: float32 [8, 512], P(None, ('nodes', 'fsdp')), may hold values from 9.765625e-07 to 9.765625e-06
Outputs:
- updated_proj: float32 [5, 512, 512], P(None, ('nodes', 'fsdp'))
- updated_ffn: float32 [2, 512, 2048], P(None, ('nodes', 'fsdp'))
- updated_vector: float32 [8, 512], P(None, ('nodes', 'fsdp'))
- mean_proj: float32 [5, 512, 512], P(None, ('nodes', 'fsdp'))
- mean_ffn: float32 [2, 512, 2048], P(None, ('nodes', 'fsdp'))
- mean_vector: float32 [8, 512], P(None, ('nodes', 'fsdp'))
- square_proj: float32 [5, 512, 512], P(None, ('nodes', 'fsdp'))
- square_ffn: float32 [2, 512, 2048], P(None, ('nodes', 'fsdp'))
- square_vector: float32 [8, 512], P(None, ('nodes', 'fsdp'))
- copy_proj: bfloat16 [5, 512, 512], P(None, ('nodes', 'fsdp'))
- copy_ffn: bfloat16 [2, 512, 2048], P(None, ('nodes', 'fsdp'))
- copy_vector: bfloat16 [8, 512], P(None, ('nodes', 'fsdp'))
- norm_pairs: float32 [15, 2], replicated
- stream_scale: float32 [4], replicated
- train_loss: float32 [], replicated
Inputs may be any that keep to these rules, and one draw needn't show every extreme that they name: `block_counts`: live slots of a device come first; one device has 12 live blocks and one has a single live block. `neighbours`: each entry names a live slot of the device it refers to.
All inputs are finite; a program needn't handle non-finite values. No bound on the sum of `node_mask` on one device may be relied on, other than what follows from the above.
Results may differ from a plain program's by a relative error of at most 0.0015.
The roundings to bfloat16 on the way count: a program that leaves them out, or rounds other values in their place, can miss the bound.
Values may be sent and summed in bfloat16 or wider, within the bound.
No kernel may reach another device: no remote copies, remote signals or barrier semaphores. Data moves between devices by JAX's collectives and lax.ppermute only.
A program may use at most 320 MiB of HBM per device.

v0:
```python
import jax
import jax.numpy as jnp
from jax import lax
from jax.sharding import PartitionSpec as P

H = 8
HD = 64
STEP = 10
NTYPES = 64


norm_eps = 1e-05
adam_eps = 1e-06
beta_first = 0.9
beta_second = 0.999
decay_rate = 0.01
learn_rate = 0.2
mask_fill = 1000000000.0
per_step = 4
precise = lax.Precision.HIGHEST


def passed_along(value, axis, steps):
    count = lax.axis_size(axis)
    pairs = [(source, (source + steps) % count) for source in range(count)]
    return lax.ppermute(value, axis, pairs)


def layer_norm(values, gain_row, shift_row):
    center = values - jnp.mean(values, -1, keepdims=True)
    spread = jnp.mean(center * center, -1, keepdims=True)
    return center * lax.rsqrt(spread + norm_eps) * gain_row + shift_row


def head_out(values, gain_row, shift_row, weight_row):
    return jnp.sum(layer_norm(values, gain_row, shift_row) * weight_row, -1)


def lamb_parts(weight, gradient, moment_one, moment_two, axes_list):
    mean_new = beta_first * moment_one + (1.0 - beta_first) * gradient
    square_new = beta_second * moment_two + (1.0 - beta_second) * gradient * gradient
    corrected = (
        mean_new
        / (1.0 - beta_first**STEP)
        / (jnp.sqrt(square_new / (1.0 - beta_second**STEP)) + adam_eps)
    )
    direction = corrected + decay_rate * weight
    return (
        mean_new,
        square_new,
        direction,
        jnp.sum(weight * weight, axes_list),
        jnp.sum(direction * direction, axes_list),
    )


def fetch_keys(packed, key_mask, span_count, again):
    got_values = []
    got_masks = []
    for shift_by in (1, -1, span_count // 4, span_count // 2):
        if again:
            moved = passed_along((packed, key_mask), "nodes", shift_by)
        else:
            moved = passed_along((packed, key_mask), "nodes", shift_by)
        got_values.append(moved[0])
        got_masks.append(moved[1])
    return (jnp.concatenate(got_values, 0), jnp.concatenate(got_masks, 0))


def group_keys(start_at, packed, key_mask, remote_kv, remote_mask, choose_all, slot_count):
    listed = choose_all.shape[1]
    own_keys = lax.dynamic_slice_in_dim(packed, start_at, per_step, 0)[:, None]
    own_mask = lax.dynamic_slice_in_dim(key_mask, start_at, per_step, 0)[:, None]
    chosen = lax.dynamic_slice_in_dim(choose_all, start_at, per_step, 0)
    offset_rows = jnp.arange(listed, dtype=jnp.int32) // 2 * slot_count
    flat_index = (chosen + offset_rows[None, :]).reshape(-1)
    far_keys = jnp.take(remote_kv, flat_index, axis=0).reshape(
        (per_step, listed) + remote_kv.shape[1:]
    )
    far_mask = jnp.take(remote_mask, flat_index, axis=0).reshape(
        (per_step, listed) + remote_mask.shape[1:]
    )
    return (
        jnp.concatenate([own_keys, far_keys], 1),
        jnp.concatenate([own_mask, far_mask], 1),
        flat_index,
    )


def split_keys(keys_all):
    half_width = keys_all.shape[-1] // 2
    head_shape = keys_all.shape[:3] + (H, HD)
    return (
        keys_all[..., :half_width].reshape(head_shape),
        keys_all[..., half_width:].reshape(head_shape),
    )


def scores_of(query, key_part, key_valid, bias_part):
    product = jnp.einsum(
        "bqhd,bjkhd->bhqjk", query, key_part, preferred_element_type=jnp.float32
    ) * HD ** (-0.5)
    return (
        product
        + bias_part[:, :, None, :, None]
        + (key_valid.astype(jnp.float32)[:, None, None, :, :] - 1.0) * mask_fill
    )


def per_device(
    features,
    targets,
    node_mask,
    block_counts,
    neighbours,
    edge_types,
    proj_weights,
    ffn_weights,
    vector_params,
    proj_mean,
    ffn_mean,
    vector_mean,
    proj_square,
    ffn_square,
    vector_square,
):
    span_count = lax.axis_size("nodes")
    slot_count = neighbours.shape[0]
    row_count, model_width = features.shape
    block_len = row_count // slot_count
    live_slots = (jnp.arange(slot_count) < block_counts[0]).astype(jnp.float32)
    valid_nodes = node_mask.astype(jnp.float32).reshape(slot_count, block_len) * live_slots[:, None]
    valid_rows = valid_nodes.reshape(row_count)
    local_count = jnp.sum(valid_rows)
    low_proj, low_ffn, low_vector = (
        lax.all_gather(proj_weights.astype(jnp.bfloat16), ("nodes", "fsdp"), axis=1, tiled=True),
        lax.all_gather(ffn_weights.astype(jnp.bfloat16), ("nodes", "fsdp"), axis=1, tiled=True),
        lax.all_gather(vector_params.astype(jnp.bfloat16), ("nodes", "fsdp"), axis=1, tiled=True),
    )
    gain_rows = low_vector.astype(jnp.float32)
    type_table = gain_rows[7].reshape(NTYPES, H)
    type_onehot = (
        edge_types[:, :, None] == jnp.arange(NTYPES, dtype=jnp.int32)[None, None, :]
    ).astype(jnp.float32)
    pair_bias = jnp.einsum("sjt,th->shj", type_onehot, type_table, precision=precise)
    base = jnp.dot(features, low_proj[0], preferred_element_type=jnp.float32)
    normed_one, norm_one_back = jax.vjp(layer_norm, base, gain_rows[0], gain_rows[1])
    attn_in = normed_one.astype(jnp.bfloat16)
    projected = jnp.einsum(
        "rd,kde->kre", attn_in, low_proj[1:4], preferred_element_type=jnp.float32
    ).astype(jnp.bfloat16)
    queries = projected[0].reshape(slot_count, block_len, H, HD)
    packed = jnp.concatenate([projected[1], projected[2]], -1).reshape(
        slot_count, block_len, 2 * model_width
    )
    key_mask = valid_nodes.astype(jnp.bfloat16)
    remote_kv, remote_mask = fetch_keys(packed, key_mask, span_count, False)
    upper = slot_count // per_step

    def forward_group(group_index, carry):
        outs_acc, mass_acc = carry
        start_at = group_index * per_step
        keys_all, key_valid, flat_index = group_keys(
            start_at, packed, key_mask, remote_kv, remote_mask, neighbours, slot_count
        )
        key_part, value_part = split_keys(keys_all)
        query = lax.dynamic_slice_in_dim(queries, start_at, per_step, 0)
        bias_part = lax.dynamic_slice_in_dim(pair_bias, start_at, per_step, 0)
        scores = scores_of(query, key_part, key_valid, bias_part)
        highest = jnp.max(scores, axis=(3, 4), keepdims=True)
        expanded = jnp.exp(scores - highest)
        mass_sum = jnp.sum(expanded, axis=(3, 4), keepdims=True)
        probs = (expanded / mass_sum).astype(jnp.bfloat16)
        attended = jnp.einsum(
            "bhqjk,bjkhd->bqhd", probs, value_part, preferred_element_type=jnp.float32
        ).astype(jnp.bfloat16)
        log_sum = (highest + jnp.log(mass_sum))[..., 0, 0]
        return (
            lax.dynamic_update_slice_in_dim(outs_acc, attended, start_at, 0),
            lax.dynamic_update_slice_in_dim(mass_acc, log_sum, start_at, 0),
        )

    attn_out, log_mass = lax.fori_loop(
        0,
        upper,
        forward_group,
        (
            jnp.zeros((slot_count, block_len, H, HD), jnp.bfloat16),
            jnp.zeros((slot_count, H, block_len), jnp.float32),
        ),
    )
    attn_rows = attn_out.reshape(row_count, model_width)
    attn_y = jnp.dot(attn_rows, low_proj[4], preferred_element_type=jnp.float32)
    middle = base + attn_y
    normed_two, norm_two_back = jax.vjp(layer_norm, middle, gain_rows[2], gain_rows[3])
    ffn_in = normed_two.astype(jnp.bfloat16)
    hidden_pre = jnp.dot(ffn_in, low_ffn[0], preferred_element_type=jnp.float32)
    hidden_act, gelu_back = jax.vjp(jax.nn.gelu, hidden_pre)
    hidden = hidden_act.astype(jnp.bfloat16)
    ffn_y = lax.dot_general(
        hidden, low_ffn[1], (((1,), (1,)), ((), ())), preferred_element_type=jnp.float32
    )
    final = middle + ffn_y
    predict, head_back = jax.vjp(head_out, final, gain_rows[4], gain_rows[5], gain_rows[6])
    error = predict - targets
    local_sums = jnp.stack(
        [jnp.sum(valid_rows * error * error)]
        + [jnp.sum(valid_rows[:, None] * piece * piece) for piece in (middle, attn_y, final, ffn_y)]
    )
    node_total, stat_sums = lax.psum((local_count, local_sums), ("nodes", "fsdp"))
    low_proj, low_ffn, low_vector = (
        lax.all_gather(proj_weights.astype(jnp.bfloat16), ("nodes", "fsdp"), axis=1, tiled=True),
        lax.all_gather(ffn_weights.astype(jnp.bfloat16), ("nodes", "fsdp"), axis=1, tiled=True),
        lax.all_gather(vector_params.astype(jnp.bfloat16), ("nodes", "fsdp"), axis=1, tiled=True),
    )
    remote_kv, remote_mask = fetch_keys(packed, key_mask, span_count, True)
    grad_pred = 2.0 * valid_rows * error / node_total
    grad_final, grad_gain_f, grad_shift_f, grad_head = head_back(grad_pred)
    grad_ffn_y = grad_final.astype(jnp.bfloat16)
    grad_down = lax.dot_general(
        grad_ffn_y, hidden, (((0,), (0,)), ((), ())), preferred_element_type=jnp.float32
    )
    grad_hidden = jnp.dot(grad_ffn_y, low_ffn[1], preferred_element_type=jnp.float32)
    grad_pre = gelu_back(grad_hidden)[0].astype(jnp.bfloat16)
    grad_up = lax.dot_general(
        ffn_in, grad_pre, (((0,), (0,)), ((), ())), preferred_element_type=jnp.float32
    )
    grad_ffn_in = lax.dot_general(
        grad_pre, low_ffn[0], (((1,), (1,)), ((), ())), preferred_element_type=jnp.float32
    )
    grad_mid_norm, grad_gain_two, grad_shift_two = norm_two_back(grad_ffn_in)
    grad_middle = grad_final + grad_mid_norm
    grad_attn_y = grad_middle.astype(jnp.bfloat16)
    grad_out_proj = lax.dot_general(
        attn_rows, grad_attn_y, (((0,), (0,)), ((), ())), preferred_element_type=jnp.float32
    )
    grad_attn = (
        lax.dot_general(
            grad_attn_y, low_proj[4], (((1,), (1,)), ((), ())), preferred_element_type=jnp.float32
        )
        .astype(jnp.bfloat16)
        .reshape(slot_count, block_len, H, HD)
    )

    def backward_group(group_index, carry):
        grad_query, grad_local, grad_remote, grad_bias = carry
        start_at = group_index * per_step
        keys_all, key_valid, flat_index = group_keys(
            start_at, packed, key_mask, remote_kv, remote_mask, neighbours, slot_count
        )
        key_part, value_part = split_keys(keys_all)
        query = lax.dynamic_slice_in_dim(queries, start_at, per_step, 0)
        bias_part = lax.dynamic_slice_in_dim(pair_bias, start_at, per_step, 0)
        grad_out = lax.dynamic_slice_in_dim(grad_attn, start_at, per_step, 0)
        log_sum = lax.dynamic_slice_in_dim(log_mass, start_at, per_step, 0)
        scores = scores_of(query, key_part, key_valid, bias_part)
        probs = jnp.exp(scores - log_sum[:, :, :, None, None])
        low_probs = probs.astype(jnp.bfloat16)
        grad_probs = jnp.einsum(
            "bqhd,bjkhd->bhqjk", grad_out, value_part, preferred_element_type=jnp.float32
        )
        inner = jnp.sum(probs * grad_probs, axis=(3, 4), keepdims=True)
        grad_scores = probs * (grad_probs - inner)
        low_scores = grad_scores.astype(jnp.bfloat16)
        bias_grad = jnp.sum(grad_scores, axis=(2, 4))
        query_grad = jnp.einsum(
            "bhqjk,bjkhd->bqhd", low_scores, key_part, preferred_element_type=jnp.float32
        ) * HD ** (-0.5)
        key_grad = jnp.einsum(
            "bhqjk,bqhd->bjkhd", low_scores, query, preferred_element_type=jnp.float32
        ) * HD ** (-0.5)
        value_grad = jnp.einsum(
            "bhqjk,bqhd->bjkhd", low_probs, grad_out, preferred_element_type=jnp.float32
        )
        pair_grad = jnp.concatenate(
            [
                key_grad.reshape(key_grad.shape[:3] + (-1,)),
                value_grad.reshape(value_grad.shape[:3] + (-1,)),
            ],
            -1,
        )
        grad_query = lax.dynamic_update_slice_in_dim(grad_query, query_grad, start_at, 0)
        grad_local = lax.dynamic_update_slice_in_dim(grad_local, pair_grad[:, 0], start_at, 0)
        grad_remote = grad_remote.at[flat_index].add(
            pair_grad[:, 1:].reshape((-1,) + pair_grad.shape[2:])
        )
        grad_bias = lax.dynamic_update_slice_in_dim(grad_bias, bias_grad, start_at, 0)
        return (grad_query, grad_local, grad_remote, grad_bias)

    start_state = (
        jnp.zeros((slot_count, block_len, H, HD), jnp.float32),
        jnp.zeros((slot_count, block_len, 2 * model_width), jnp.float32),
        jnp.zeros((4 * slot_count, block_len, 2 * model_width), jnp.float32),
        jnp.zeros((slot_count, H, neighbours.shape[1] + 1), jnp.float32),
    )
    grad_query, grad_local, grad_remote, grad_bias = lax.fori_loop(
        0, upper, backward_group, start_state
    )
    for part_index, shift_by in enumerate((1, -1, span_count // 4, span_count // 2)):
        piece = grad_remote[part_index * slot_count : (part_index + 1) * slot_count].astype(
            jnp.bfloat16
        )
        grad_local = grad_local + passed_along(piece, "nodes", -shift_by).astype(jnp.float32)
    grad_pairs = grad_local.astype(jnp.bfloat16).reshape(row_count, 2 * model_width)
    grad_proj_rows = jnp.stack(
        [
            grad_query.astype(jnp.bfloat16).reshape(row_count, model_width),
            grad_pairs[:, :model_width],
            grad_pairs[:, model_width:],
        ]
    )
    grad_qkv = jnp.einsum(
        "rd,kre->kde", attn_in, grad_proj_rows, preferred_element_type=jnp.float32
    )
    grad_attn_in = jnp.einsum(
        "kre,kde->rd", grad_proj_rows, low_proj[1:4], preferred_element_type=jnp.float32
    )
    grad_base_norm, grad_gain_one, grad_shift_one = norm_one_back(grad_attn_in)
    grad_base = (grad_middle + grad_base_norm).astype(jnp.bfloat16)
    grad_encoder = lax.dot_general(
        features, grad_base, (((0,), (0,)), ((), ())), preferred_element_type=jnp.float32
    )
    grad_table = jnp.einsum("sjt,shj->th", type_onehot, grad_bias, precision=precise)
    grad_proj_all = jnp.concatenate([grad_encoder[None], grad_qkv, grad_out_proj[None]], 0)
    grad_ffn_all = jnp.stack([grad_up, grad_down])
    grad_vector_all = jnp.stack(
        [
            grad_gain_one,
            grad_shift_one,
            grad_gain_two,
            grad_shift_two,
            grad_gain_f,
            grad_shift_f,
            grad_head,
            grad_table.reshape(model_width),
        ]
    )
    shard_proj, shard_ffn, shard_vector = (
        lax.psum_scatter(grad_proj_all, ("nodes", "fsdp"), scatter_dimension=1, tiled=True),
        lax.psum_scatter(grad_ffn_all, ("nodes", "fsdp"), scatter_dimension=1, tiled=True),
        lax.psum_scatter(grad_vector_all, ("nodes", "fsdp"), scatter_dimension=1, tiled=True),
    )
    proj_parts = lamb_parts(proj_weights, shard_proj, proj_mean, proj_square, (1, 2))
    ffn_parts = lamb_parts(ffn_weights, shard_ffn, ffn_mean, ffn_square, (1, 2))
    vector_parts = lamb_parts(vector_params, shard_vector, vector_mean, vector_square, (1,))
    local_squares = jnp.stack(
        [
            jnp.concatenate([proj_parts[3], ffn_parts[3], vector_parts[3]]),
            jnp.concatenate([proj_parts[4], ffn_parts[4], vector_parts[4]]),
        ],
        1,
    )
    norm_squares = lax.psum(local_squares, ("nodes", "fsdp"))
    norm_pairs = jnp.sqrt(norm_squares)
    ratio = norm_pairs[:, 0] / norm_pairs[:, 1]
    updated_proj = proj_weights - learn_rate * ratio[0:5, None, None] * proj_parts[2]
    updated_ffn = ffn_weights - learn_rate * ratio[5:7, None, None] * ffn_parts[2]
    updated_vector = vector_params - learn_rate * ratio[7:15, None] * vector_parts[2]
    train_loss = stat_sums[0] / node_total
    stream_scale = jnp.sqrt(stat_sums[1:] / (node_total * model_width))
    return (
        updated_proj,
        updated_ffn,
        updated_vector,
        proj_parts[0],
        ffn_parts[0],
        vector_parts[0],
        proj_parts[1],
        ffn_parts[1],
        vector_parts[1],
        updated_proj.astype(jnp.bfloat16),
        updated_ffn.astype(jnp.bfloat16),
        updated_vector.astype(jnp.bfloat16),
        norm_pairs,
        stream_scale,
        train_loss,
    )


def solution(mesh):
    placed = (
        P(("nodes", "fsdp"), None),
        P(("nodes", "fsdp")),
        P(("nodes", "fsdp")),
        P(("nodes", "fsdp")),
        P(("nodes", "fsdp"), None),
        P(("nodes", "fsdp"), None),
        P(None, ("nodes", "fsdp"), None),
        P(None, ("nodes", "fsdp"), None),
        P(None, ("nodes", "fsdp")),
        P(None, ("nodes", "fsdp"), None),
        P(None, ("nodes", "fsdp"), None),
        P(None, ("nodes", "fsdp")),
        P(None, ("nodes", "fsdp"), None),
        P(None, ("nodes", "fsdp"), None),
        P(None, ("nodes", "fsdp")),
    )
    return jax.shard_map(
        per_device,
        mesh=mesh,
        in_specs=placed,
        out_specs=(
            P(None, ("nodes", "fsdp"), None),
            P(None, ("nodes", "fsdp"), None),
            P(None, ("nodes", "fsdp")),
            P(None, ("nodes", "fsdp"), None),
            P(None, ("nodes", "fsdp"), None),
            P(None, ("nodes", "fsdp")),
            P(None, ("nodes", "fsdp"), None),
            P(None, ("nodes", "fsdp"), None),
            P(None, ("nodes", "fsdp")),
            P(None, ("nodes", "fsdp"), None),
            P(None, ("nodes", "fsdp"), None),
            P(None, ("nodes", "fsdp")),
            P(),
            P(),
            P(),
        ),
        check_vma=False,
    )
```

profile of v0, /device:TPU:10, one launch (start us, length us, event | category | flops | bytes accessed | tf_op | source)
XLA Modules:
  0.0 2136.7 jit_solution(7957681409180844476)
XLA Ops:
  9.7 31.0 %all-gather = bf16[32,16,8]{1,2,0:T(8,128)(2,1)S(1)} all-gather(bf16[1,16,8]{1,2,0:T(8,128)(2,1)S(1)} %convert_bitcast_fusion.1), channel_id=1, replica_groups=mesh['nodes'=16,'fsdp'=2] {'nodes','fsdp'}, dimensions={0}, use_global_device_ids=true | all-gather | bytes 8448 | tf_op jit(solution)/shard_map/all_gather | solution.py:138
  41.4 27.7 %all-gather.4.cloned.1.call-done = bf16[5,512,512]{2,1,0:T(8,128)(2,1)} async-done(((bf16[5,16,512]{2,1,0:T(8,128)(2,1)}), bf16[5,512,512]{2,1,0:T(8,128)(2,1)}) %all-gather.4.cloned.1.call-update) | async-done | bytes 2621456 | tf_op jit(solution)/shard_map/all_gather | solution.py:136
  99.8 200.7 %collective-permute-done.7 = bf16[12,128]{1,0:T(8,128)(2,1)S(1)} collective-permute-done((bf16[12,128]{1,0:T(8,128)(2,1)S(1)}, bf16[12,128]{1,0:T(8,128)(2,1)S(1)}, u32[]{:S(2)}, u32[]{:S(2)}) %collective-permute-start.7) | collective-permute-done | bytes 3104 | tf_op jit(solution)/shard_map/ppermute | solution.py:26
  306.4 73.3 %collective-permute-start.5 = (bf16[12,128]{1,0:T(8,128)(2,1)S(1)}, bf16[12,128]{1,0:T(8,128)(2,1)S(1)}, u32[]{:S(2)}, u32[]{:S(2)}) collective-permute-start(bf16[12,128]{1,0:T(8,128)(2,1)S(1)} %fusion.121), channel_id=1, source_target_pairs={{0,30},{2,0},{4,2},{6,4},{8,6},{10,8},{12,10},{14,12},{16,14},{18,... | collective-permute-start | bytes 9224 | tf_op jit(solution)/shard_map/ppermute | solution.py:26
  411.8 168.1 %while.38 = (s32[]{:T(128)}, bf16[12,128,8,64]{1,0,3,2:T(8,128)(2,1)}, f32[12,8,128]{2,1,0:T(8,128)S(1)}, bf16[12,128,1024]{1,2,0:T(8,128)(2,1)}, s32[12,8]{1,0:...) while((s32[]{:T(128)}, ...), condition=%wide.region_8.11_spmd, body=%wide.region_5.10_spmd.sunk | while | flops 1302098304 | bytes 139722992 | solution.py:183
  613.0 44.9 %psum.21 = f32[]{:T(128)} all-reduce(f32[]{:T(128)} %get-tuple-element.764), channel_id=1, replica_groups=mesh['nodes'=16,'fsdp'=2] {'nodes','fsdp'}, use_global_device_ids=true, to_apply=%region_15.18 | all-reduce | flops 1 | bytes 8 | tf_op jit(solution)/shard_map/psum | solution.py:210
  664.4 14.8 fusion.82
  728.7 602.7 %while.39 = (s32[]{:T(128)}, bf16[12,128,8,64]{1,3,2,0:T(8,128)(2,1)}, f32[12,128,1024]{2,1,0:T(8,128)}, f32[48,128,1024]{2,1,0:T(8,128)}, f32[12,8,9]{2,1,0:T(8...) while((s32[]{:T(128)}, ...), condition=%wide.region_24.27_spmd, body=%wide.region_20.0_spmd.sunk | while | flops 3144183808 | bytes 684476800 | solution.py:296
  798.5 20.2 multiply_reduce_fusion.18
  818.8 14.6 fusion.201
  870.4 17.5 copy.364
  894.0 35.6 %scatter_fusion = f32[48,128,1024]{2,1,0:T(8,128)} fusion(f32[48,128,1024]{2,1,0:T(8,128)} %get-tuple-element.1102, s32[32]{0:T(128)S(1)} %fusion.204, f32[32,128,1024]{2,1,0:T(8,128)} %copy.364), kind=kCustom, calls=%fused_computation.4.clone.1 | custom fusion | flops 4194304 | bytes 50331776 | tf_op jit(solution)/shard_map/while/body/eval_jaxpr/scatter-add | solution.py:284
  999.0 20.2 multiply_reduce_fusion.18
  1070.9 17.5 copy.364
  1094.5 36.1 %scatter_fusion = f32[48,128,1024]{2,1,0:T(8,128)} fusion(f32[48,128,1024]{2,1,0:T(8,128)} %get-tuple-element.1102, s32[32]{0:T(128)S(1)} %fusion.204, f32[32,128,1024]{2,1,0:T(8,128)} %copy.364), kind=kCustom, calls=%fused_computation.4.clone.1 | custom fusion | flops 4194304 | bytes 50331776 | tf_op jit(solution)/shard_map/while/body/eval_jaxpr/scatter-add | solution.py:284
  1200.0 20.2 multiply_reduce_fusion.18
  1271.9 17.5 copy.364
  1295.5 35.7 %scatter_fusion = f32[48,128,1024]{2,1,0:T(8,128)} fusion(f32[48,128,1024]{2,1,0:T(8,128)} %get-tuple-element.1102, s32[32]{0:T(128)S(1)} %fusion.204, f32[32,128,1024]{2,1,0:T(8,128)} %copy.364), kind=kCustom, calls=%fused_computation.4.clone.1 | custom fusion | flops 4194304 | bytes 50331776 | tf_op jit(solution)/shard_map/while/body/eval_jaxpr/scatter-add | solution.py:284
  1362.4 55.5 %collective-permute-done.8 = bf16[12,128,1024]{2,1,0:T(8,128)(2,1)} collective-permute-done((bf16[12,128,1024]{2,1,0:T(8,128)(2,1)}, bf16[12,128,1024]{2,1,0:T(8,128)(2,1)}, u32[]{:S(2)}, u32[]{:S(2)}) %collective-permute-start.8) | collective-permute-done | bytes 3145760 | tf_op jit(solution)/shard_map/ppermute | solution.py:26
  1417.9 128.6 %collective-permute-done.11 = bf16[12,128,1024]{2,1,0:T(8,128)(2,1)} collective-permute-done((bf16[12,128,1024]{2,1,0:T(8,128)(2,1)}, bf16[12,128,1024]{2,1,0:T(8,128)(2,1)}, u32[]{:S(2)}, u32[]{:S(2)}) %collective-permute-start.11) | collective-permute-done | bytes 3145760 | tf_op jit(solution)/shard_map/ppermute | solution.py:26
  1623.0 141.0 %reduce-scatter.10.cloned.1.call-done = f32[16,8]{1,0:T(8,128)} async-done(((f32[512,8]{1,0:T(8,128)}), f32[16,8]{1,0:T(8,128)}) %reduce-scatter.10.cloned.1.call-update) | async-done | bytes 528
  1765.0 147.0 %reduce-scatter.6.cloned.1.call-done = f32[5,16,512]{2,0,1:T(8,128)} async-done(((f32[5,512,512]{2,0,1:T(8,128)}), f32[5,16,512]{2,0,1:T(8,128)}) %reduce-scatter.6.cloned.1.call-update) | async-done | bytes 163856 | tf_op jit(solution)/shard_map/reduce_scatter | solution.py:339
  1913.3 146.9 %reduce-scatter.8.cloned.1.call-done = f32[2,16,2048]{2,1,0:T(8,128)} async-done(((f32[2,512,2048]{2,1,0:T(8,128)}), f32[2,16,2048]{2,1,0:T(8,128)}) %reduce-scatter.8.cloned.1.call-update) | async-done | bytes 262160 | tf_op jit(solution)/shard_map/reduce_scatter | solution.py:340
  2062.2 62.7 %all-reduce = (f32[15,2]{0,1:T(2,128)S(1)}, f32[5]{0:T(128)S(1)}) all-reduce(f32[15,2]{0,1:T(2,128)S(1)} %pad_maximum_fusion.12, f32[5]{0:T(128)S(1)} %stack.70), channel_id=1, replica_groups=mesh['nodes'=16,'fsdp'=2] {'nodes','fsdp'}, use_global_device_ids=true, to_apply=%region_40.43 | all-reduce | flops 35 | bytes 280 | tf_op jit(solution)/shard_map/psum | solution.py:353
  (566 shorter events, 807.9 us)
Async XLA Ops:
  7.2 61.9 %all-gather.4.cloned.1.call-start = ((), (), s32[]{:S(2)}) async-start(), calls=%async_computation.3 | async-start | bytes 2703360 | tf_op jit(solution)/shard_map/all_gather | solution.py:136
  8.9 578.5 %all-gather.6.cloned.1.call-start = ((), (), s32[]{:S(2)}) async-start(), calls=%async_computation.4 | async-start | bytes 4325376 | tf_op jit(solution)/shard_map/all_gather | solution.py:137
  87.7 296.3 %copy-start.85 = (s32[12,8]{0,1:T(8,128)S(1)}, s32[12,8]{0,1:T(8,128)}, u32[]{:S(2)}) copy-start(s32[12,8]{0,1:T(8,128)} %param.27) | copy-start | bytes 1156
  92.4 305.3 %collective-permute-start = (bf16[12,128,1024]{2,1,0:T(8,128)(2,1)}, bf16[12,128,1024]{2,1,0:T(8,128)(2,1)}, u32[]{:S(2)}, u32[]{:S(2)}) collective-permute-start(bf16[12,128,1024]{2,1,0:T(8,128)(2,1)} %copy.198), channel_id=1, source_target_pairs={{0,2},{2,4},{4,6},{6,8},{8,10},{10,12},{12,14},{14,16},{16,18},{18... | collective-permute-start | bytes 9437192 | tf_op jit(solution)/shard_map/ppermute | solution.py:26
  93.9 306.1 %collective-permute-start.1 = (bf16[12,128,1024]{2,1,0:T(8,128)(2,1)}, bf16[12,128,1024]{2,1,0:T(8,128)(2,1)}, u32[]{:S(2)}, u32[]{:S(2)}) collective-permute-start(bf16[12,128,1024]{2,1,0:T(8,128)(2,1)} %copy.198), channel_id=1, source_target_pairs={{0,30},{2,0},{4,2},{6,4},{8,6},{10,8},{12,10},{14,12},{16,14},{18,... | collective-permute-start | bytes 9437192 | tf_op jit(solution)/shard_map/ppermute | solution.py:26
  94.5 307.8 %collective-permute-start.2 = (bf16[12,128,1024]{2,1,0:T(8,128)(2,1)}, bf16[12,128,1024]{2,1,0:T(8,128)(2,1)}, u32[]{:S(2)}, u32[]{:S(2)}) collective-permute-start(bf16[12,128,1024]{2,1,0:T(8,128)(2,1)} %copy.198), channel_id=1, source_target_pairs={{0,8},{2,10},{4,12},{6,14},{8,16},{10,18},{12,20},{14,22},{16,24},... | collective-permute-start | bytes 9437192 | tf_op jit(solution)/shard_map/ppermute | solution.py:26
  95.3 309.2 %collective-permute-start.3 = (bf16[12,128,1024]{2,1,0:T(8,128)(2,1)}, bf16[12,128,1024]{2,1,0:T(8,128)(2,1)}, u32[]{:S(2)}, u32[]{:S(2)}) collective-permute-start(bf16[12,128,1024]{2,1,0:T(8,128)(2,1)} %copy.198), channel_id=1, source_target_pairs={{0,16},{2,18},{4,20},{6,22},{8,24},{10,26},{12,28},{14,30},{16,0},... | collective-permute-start | bytes 9437192 | tf_op jit(solution)/shard_map/ppermute | solution.py:26
  99.1 201.5 %collective-permute-start.7 = (bf16[12,128]{1,0:T(8,128)(2,1)S(1)}, bf16[12,128]{1,0:T(8,128)(2,1)S(1)}, u32[]{:S(2)}, u32[]{:S(2)}) collective-permute-start(bf16[12,128]{1,0:T(8,128)(2,1)S(1)} %fusion.121), channel_id=1, source_target_pairs={{0,16},{2,18},{4,20},{6,22},{8,24},{10,26},{12,28},{14,30},{16,0},... | collective-permute-start | bytes 9224 | tf_op jit(solution)/shard_map/ppermute | solution.py:26
  99.8 1664.3 %reduce-scatter.10.cloned.1.call-start = ((), (), s32[]{:S(2)}) async-start(), calls=%async_computation.7 | async-start | bytes 270336
  300.5 5.9 collective-permute-start.6
  306.4 74.6 %collective-permute-start.5 = (bf16[12,128]{1,0:T(8,128)(2,1)S(1)}, bf16[12,128]{1,0:T(8,128)(2,1)S(1)}, u32[]{:S(2)}, u32[]{:S(2)}) collective-permute-start(bf16[12,128]{1,0:T(8,128)(2,1)S(1)} %fusion.121), channel_id=1, source_target_pairs={{0,30},{2,0},{4,2},{6,4},{8,6},{10,8},{12,10},{14,12},{16,14},{18,... | collective-permute-start | bytes 9224 | tf_op jit(solution)/shard_map/ppermute | solution.py:26
  381.1 7.0 collective-permute-start.4
  1345.7 72.2 %collective-permute-start.8 = (bf16[12,128,1024]{2,1,0:T(8,128)(2,1)}, bf16[12,128,1024]{2,1,0:T(8,128)(2,1)}, u32[]{:S(2)}, u32[]{:S(2)}) collective-permute-start(bf16[12,128,1024]{2,1,0:T(8,128)(2,1)} %get-tuple-element.845), channel_id=1, source_target_pairs={{0,30},{2,0},{4,2},{6,4},{8,6},{10,8},{12,10},{14,12},{16,14},{18,... | collective-permute-start | bytes 9437192 | tf_op jit(solution)/shard_map/ppermute | solution.py:26
  1345.7 200.8 %collective-permute-start.11 = (bf16[12,128,1024]{2,1,0:T(8,128)(2,1)}, bf16[12,128,1024]{2,1,0:T(8,128)(2,1)}, u32[]{:S(2)}, u32[]{:S(2)}) collective-permute-start(bf16[12,128,1024]{2,1,0:T(8,128)(2,1)} %get-tuple-element.846), channel_id=1, source_target_pairs={{0,16},{2,18},{4,20},{6,22},{8,24},{10,26},{12,28},{14,30},{16,0},... | collective-permute-start | bytes 9437192 | tf_op jit(solution)/shard_map/ppermute | solution.py:26
  1345.7 201.9 %collective-permute-start.10 = (bf16[12,128,1024]{2,1,0:T(8,128)(2,1)}, bf16[12,128,1024]{2,1,0:T(8,128)(2,1)}, u32[]{:S(2)}, u32[]{:S(2)}) collective-permute-start(bf16[12,128,1024]{2,1,0:T(8,128)(2,1)} %get-tuple-element.847), channel_id=1, source_target_pairs={{0,24},{2,26},{4,28},{6,30},{8,0},{10,2},{12,4},{14,6},{16,8},{18,... | collective-permute-start | bytes 9437192 | tf_op jit(solution)/shard_map/ppermute | solution.py:26
  1346.6 201.0 %collective-permute-start.9 = (bf16[12,128,1024]{2,1,0:T(8,128)(2,1)}, bf16[12,128,1024]{2,1,0:T(8,128)(2,1)}, u32[]{:S(2)}, u32[]{:S(2)}) collective-permute-start(bf16[12,128,1024]{2,1,0:T(8,128)(2,1)} %get-tuple-element.848), channel_id=1, source_target_pairs={{0,2},{2,4},{4,6},{6,8},{8,10},{10,12},{12,14},{14,16},{16,18},{18... | collective-permute-start | bytes 9437192 | tf_op jit(solution)/shard_map/ppermute | solution.py:26
  1584.1 327.9 %reduce-scatter.6.cloned.1.call-start = ((), (), s32[]{:S(2)}) async-start(), calls=%async_computation.5 | async-start | bytes 8650752 | tf_op jit(solution)/shard_map/reduce_scatter | solution.py:339
  1598.9 461.3 %reduce-scatter.8.cloned.1.call-start = ((), (), s32[]{:S(2)}) async-start(), calls=%async_computation.6 | async-start | bytes 8650752 | tf_op jit(solution)/shard_map/reduce_scatter | solution.py:340
  1619.6 292.4 %copy-start.29 = (f32[5,16,512]{2,1,0:T(8,128)S(1)}, f32[5,16,512]{2,1,0:T(8,128)}, u32[]{:S(2)}) copy-start(f32[5,16,512]{2,1,0:T(8,128)} %param.29) | copy-start | bytes 491524
  1619.6 440.6 %copy-start.25 = (f32[2,16,2048]{2,1,0:T(8,128)S(1)}, f32[2,16,2048]{2,1,0:T(8,128)}, u32[]{:S(2)}) copy-start(f32[2,16,2048]{2,1,0:T(8,128)} %param.30) | copy-start | bytes 786436
  1619.6 440.6 %copy-start.39 = (f32[2,16,2048]{2,1,0:T(8,128)S(1)}, f32[2,16,2048]{2,1,0:T(8,128)}, u32[]{:S(2)}) copy-start(f32[2,16,2048]{2,1,0:T(8,128)} %param.33) | copy-start | bytes 786436
  1619.6 440.6 %copy-start.40 = (f32[2,16,2048]{2,1,0:T(8,128)S(1)}, f32[2,16,2048]{2,1,0:T(8,128)}, u32[]{:S(2)}) copy-start(f32[2,16,2048]{2,1,0:T(8,128)} %param.36) | copy-start | bytes 786436
  1765.0 363.8 %copy-start.76 = (f32[8,16]{1,0:T(8,128)}, f32[8,16]{1,0:T(8,128)S(1)}, u32[]{:S(2)}) copy-start(f32[8,16]{1,0:T(8,128)S(1)} %get-tuple-element.829) | copy-start | bytes 1540
  1765.0 363.8 %copy-start.77 = (f32[8,16]{1,0:T(8,128)}, f32[8,16]{1,0:T(8,128)S(1)}, u32[]{:S(2)}) copy-start(f32[8,16]{1,0:T(8,128)S(1)} %get-tuple-element.830) | copy-start | bytes 1540
  (124 other events, 3319.0 us)
Sparse Core Ops, SparseCore 0:
  11.5 57.5 all-gather.3
  99.9 299.6 all-gather.5
  1584.2 179.7 reduce-scatter.9
  1766.2 145.7 reduce-scatter.5
  1914.2 145.9 reduce-scatter.7
where the time goes:
time: 2150 us; the launch traced here: 2140 us
  waiting for transfers between devices  857 us (40%)
  local copies, waits for them, and re-layouts  412 us (19%)
  other arithmetic  346 us (16%)
  matrix products  275 us (13%)
  blocking collectives  139 us (6%)
  starting transfers between devices  87.9 us (4%)
    ppermute x12, waiting for transfers between devices, passed_along(): return lax.ppermute(value, axis, pairs)  394 us
    reduce_scatter x1, waiting for transfers between devices, per_device(): lax.psum_scatter(grad_proj_all, ('nodes', 'fsdp'), scatter_dimension=1, t...  147 us
    reduce_scatter x1, waiting for transfers between devices, per_device(): lax.psum_scatter(grad_ffn_all, ('nodes', 'fsdp'), scatter_dimension=1, ti...  147 us
    unnamed x6, waiting for transfers between devices  141 us
    scatter-add x3, other arithmetic, backward_group(): grad_remote.at[flat_index]  107 us
    ppermute x12, starting transfers between devices, passed_along(): return lax.ppermute(value, axis, pairs)  87.7 us
    select_n x6, local copies, waits for them, and re-layouts, group_keys(): jnp.take(remote_kv, flat_index, axis=0)  71.6 us
    psum x1, blocking collectives, per_device(): norm_squares = lax.psum(local_squares, ('nodes', 'fsdp'))  62.7 us
  transfers between devices with their start and end apart: 17, of which 11 were waited for; matrix products, arithmetic and copies ran while one was open for 12% of the time, Pallas kernels for 0%

commit v1 on v0

v1 whole, which is shorter than its diff:
```python
import functools
import jax
import jax.numpy as jnp
from jax import lax
from jax.experimental import pallas as pl
from jax.experimental.pallas import tpu as pltpu
from jax.sharding import PartitionSpec as P

H = 8
HD = 64
STEP = 10
NTYPES = 64

norm_eps = 1e-05
adam_eps = 1e-06
beta_first = 0.9
beta_second = 0.999
decay_rate = 0.01
learn_rate = 0.2
mask_fill = 1000000000.0
precise = lax.Precision.HIGHEST
both = ("nodes", "fsdp")
f32 = jnp.float32
bf16 = jnp.bfloat16
scale = HD ** (-0.5)


def passed_along(value, steps):
    count = lax.axis_size("nodes")
    pairs = [(source, (source + steps) % count) for source in range(count)]
    return lax.ppermute(value, "nodes", pairs)


def layer_norm(values, gain_row, shift_row):
    center = values - jnp.mean(values, -1, keepdims=True)
    spread = jnp.mean(center * center, -1, keepdims=True)
    return center * lax.rsqrt(spread + norm_eps) * gain_row + shift_row


def head_out(values, gain_row, shift_row, weight_row):
    return jnp.sum(layer_norm(values, gain_row, shift_row) * weight_row, -1)


def lamb_parts(weight, gradient, moment_one, moment_two, axes_list):
    mean_new = beta_first * moment_one + (1.0 - beta_first) * gradient
    square_new = beta_second * moment_two + (1.0 - beta_second) * gradient * gradient
    corrected = (
        mean_new
        / (1.0 - beta_first**STEP)
        / (jnp.sqrt(square_new / (1.0 - beta_second**STEP)) + adam_eps)
    )
    direction = corrected + decay_rate * weight
    return (
        mean_new,
        square_new,
        direction,
        jnp.sum(weight * weight, axes_list),
        jnp.sum(direction * direction, axes_list),
    )


def nn(a, b):
    return lax.dot_general(a, b, (((1,), (0,)), ((), ())), preferred_element_type=f32)


def nt(a, b):
    return lax.dot_general(a, b, (((1,), (1,)), ((), ())), preferred_element_type=f32)


def tn(a, b):
    return lax.dot_general(a, b, (((0,), (0,)), ((), ())), preferred_element_type=f32)


def encode(x_ref, w0_ref, vec_ref):
    base = nn(x_ref[...], w0_ref[0])
    normed = layer_norm(base, vec_ref[0:1], vec_ref[1:2])
    return base, normed.astype(bf16)


def local_body(x_ref, w0_ref, w1_ref, w2_ref, w3_ref, vec_ref, base_ref, a1_ref, q_ref, kv_ref):
    width = x_ref.shape[1]
    base, a1 = encode(x_ref, w0_ref, vec_ref)
    base_ref[...] = base
    a1_ref[...] = a1
    q_ref[...] = nn(a1, w1_ref[0]).astype(bf16) * jnp.asarray(scale, bf16)
    kv_ref[:, :width] = nn(a1, w2_ref[0]).astype(bf16)
    kv_ref[:, width:] = nn(a1, w3_ref[0]).astype(bf16)


def remote_body(x_ref, w0_ref, w2_ref, w3_ref, vec_ref, a1_ref, kv_ref):
    width = x_ref.shape[1]
    _, a1 = encode(x_ref, w0_ref, vec_ref)
    a1_ref[...] = a1
    kv_ref[:, :width] = nn(a1, w2_ref[0]).astype(bf16)
    kv_ref[:, width:] = nn(a1, w3_ref[0]).astype(bf16)


def project(x, weights, vectors, local):
    rows, width = x.shape
    tile = 512
    row_spec = pl.BlockSpec((tile, width), lambda i: (i, 0))
    wide_spec = pl.BlockSpec((tile, 2 * width), lambda i: (i, 0))
    used = (0, 1, 2, 3) if local else (0, 2, 3)
    weight_specs = [
        pl.BlockSpec((1, width, width), functools.partial(lambda k, i: (k, 0, 0), k)) for k in used
    ]
    outs = [jax.ShapeDtypeStruct((rows, width), bf16), jax.ShapeDtypeStruct((rows, 2 * width), bf16)]
    out_specs = [row_spec, wide_spec]
    if local:
        outs = [
            jax.ShapeDtypeStruct((rows, width), f32),
            outs[0],
            jax.ShapeDtypeStruct((rows, width), bf16),
            outs[1],
        ]
        out_specs = [row_spec, row_spec, row_spec, wide_spec]
    return pl.pallas_call(
        local_body if local else remote_body,
        grid=(rows // tile,),
        in_specs=[row_spec] + weight_specs + [pl.BlockSpec(vectors.shape, lambda i: (0, 0))],
        out_specs=out_specs,
        out_shape=outs,
        cost_estimate=pl.CostEstimate(
            flops=2 * rows * width * width * len(used),
            bytes_accessed=rows * width * 8 + len(used) * width * width * 2,
            transcendentals=rows,
        ),
        compiler_params=pltpu.CompilerParams(vmem_limit_bytes=40 << 20),
        name="project_local" if local else "project_remote",
    )(x, *([weights] * len(used)), vectors)


def split_heads(pair):
    low_half = lax.broadcasted_iota(jnp.int32, pair.shape, 1) < HD
    zero = jnp.zeros_like(pair)
    return jnp.concatenate([jnp.where(low_half, pair, zero), jnp.where(low_half, zero, pair)], 0)


def join_heads(stacked):
    half = stacked.shape[0] // 2
    upper, lower = stacked[:half], stacked[half:]
    low_half = lax.broadcasted_iota(jnp.int32, upper.shape, 1) < HD
    return jnp.where(low_half, upper, lower)


def fetch_list(block, slot, nbr_ref, own_ref, far_refs, buf, sems, listed, length):
    out = [
        pltpu.make_async_copy(own_ref.at[block], buf.at[slot, pl.ds(0, length)], sems.at[slot, 0])
    ]
    for j in range(listed):
        out.append(
            pltpu.make_async_copy(
                far_refs[j // 2].at[nbr_ref[block * listed + j]],
                buf.at[slot, pl.ds((j + 1) * length, length)],
                sems.at[slot, j + 1],
            )
        )
    return out


def forward_body(listed, slots, nbr_ref, bias_ref, q_ref, mask_ref, own_ref, r0, r1, r2, r3,
                 out_ref, lse_ref, buf, s_scr, p_scr, sems):
    block = pl.program_id(0)
    length = q_ref.shape[1]
    width = q_ref.shape[2]
    keys = (listed + 1) * length
    far = (r0, r1, r2, r3)
    fetch = functools.partial(
        fetch_list, nbr_ref=nbr_ref, own_ref=own_ref, far_refs=far, buf=buf, sems=sems,
        listed=listed, length=length,
    )

    @pl.when(block == 0)
    def _():
        for c in fetch(0, 0):
            c.start()

    @pl.when(block + 1 < slots)
    def _():
        for c in fetch(block + 1, (block + 1) % 2):
            c.start()

    slot = block % 2
    for c in fetch(block, slot):
        c.wait()
    masks = [mask_ref[block]]
    for j in range(listed):
        masks.append(mask_ref[(j // 2 + 1) * slots + nbr_ref[block * listed + j]])
    for pair in range(H // 2):
        cols = pl.ds(pair * 2 * HD, 2 * HD)
        queries = split_heads(q_ref[0, :, cols])
        s_scr[...] = nt(queries, buf[slot, :, cols])
        top = None
        for j in range(listed + 1):
            part = pl.ds(j * length, length)
            pieces = []
            for h in range(2):
                row = masks[j] + bias_ref[(block * H + pair * 2 + h) * (listed + 1) + j]
                pieces.append(s_scr[pl.ds(h * length, length), part] + row)
            piece = jnp.concatenate(pieces, 0)
            s_scr[:, part] = piece
            top = piece if top is None else jnp.maximum(top, piece)
        highest = jnp.max(top, axis=1, keepdims=True)
        mass = None
        for j in range(listed + 1):
            part = pl.ds(j * length, length)
            piece = jnp.exp(s_scr[:, part] - highest)
            s_scr[:, part] = piece
            mass = piece if mass is None else mass + piece
        total = jnp.sum(mass, axis=1, keepdims=True)
        inverse = 1.0 / total
        for j in range(listed + 1):
            part = pl.ds(j * length, length)
            p_scr[:, part] = (s_scr[:, part] * inverse).astype(bf16)
        values = buf[slot, :, pl.ds(width + pair * 2 * HD, 2 * HD)]
        out_ref[0, :, cols] = join_heads(nn(p_scr[...], values)).astype(bf16)
        lse = jnp.broadcast_to(highest + jnp.log(total), (2 * length, 128))
        lse_ref[0, :, pl.ds(pair * 2 * length, 2 * length)] = lse.T[0:1]


def attend(nbr, bias, queries, masks, own, far):
    slots, length, width = queries.shape
    listed = nbr.shape[0] // slots
    keys = (listed + 1) * length
    any_spec = pl.BlockSpec(memory_space=pl.ANY)
    return pl.pallas_call(
        functools.partial(forward_body, listed, slots),
        grid_spec=pltpu.PrefetchScalarGridSpec(
            num_scalar_prefetch=2,
            grid=(slots,),
            in_specs=[
                pl.BlockSpec((1, length, width), lambda b, *_: (b, 0, 0)),
                pl.BlockSpec(masks.shape, lambda b, *_: (0, 0, 0)),
            ]
            + [any_spec] * 5,
            out_specs=[
                pl.BlockSpec((1, length, width), lambda b, *_: (b, 0, 0)),
                pl.BlockSpec((1, 1, H * length), lambda b, *_: (b, 0, 0)),
            ],
            scratch_shapes=[
                pltpu.VMEM((2, keys, 2 * width), bf16),
                pltpu.VMEM((2 * length, keys), f32),
                pltpu.VMEM((2 * length, keys), bf16),
                pltpu.SemaphoreType.DMA((2, listed + 1)),
            ],
        ),
        out_shape=[
            jax.ShapeDtypeStruct((slots, length, width), bf16),
            jax.ShapeDtypeStruct((slots, 1, H * length), f32),
        ],
        cost_estimate=pl.CostEstimate(
            flops=4 * slots * length * keys * width * 2,
            bytes_accessed=slots * keys * width * 4,
            transcendentals=slots * length * keys * H,
        ),
        compiler_params=pltpu.CompilerParams(vmem_limit_bytes=40 << 20),
        name="attention_forward",
    )(nbr, bias, queries, masks, own, *far)


def backward_body(listed, slots, nbr_ref, bias_ref, q_ref, g_ref, lse_ref, mask_ref, own_ref,
                  r0, r1, r2, r3, dq_ref, down_ref, dfar_ref, dbias_ref,
                  buf, mcol, p_scr, g_scr, pl_scr, ds_scr, acc, sems, msems):
    step = pl.program_id(0)
    length = q_ref.shape[1]
    width = q_ref.shape[2]
    far = (r0, r1, r2, r3)
    fetch = functools.partial(
        fetch_list, nbr_ref=nbr_ref, own_ref=own_ref, far_refs=far, buf=buf, sems=sems,
        listed=listed, length=length,
    )

    def mask_list(block, slot):
        out = [
            pltpu.make_async_copy(
                mask_ref.at[block], mcol.at[slot, pl.ds(0, length)], msems.at[slot, 0]
            )
        ]
        for j in range(listed):
            out.append(
                pltpu.make_async_copy(
                    mask_ref.at[(j // 2 + 1) * slots + nbr_ref[block * listed + j]],
                    mcol.at[slot, pl.ds((j + 1) * length, length)],
                    msems.at[slot, j + 1],
                )
            )
        return out

    @pl.when(step == 0)
    def _():
        for c in fetch(0, 0) + mask_list(0, 0):
            c.start()
        for i in range(4 * slots):
            acc[i] = jnp.zeros(acc.shape[1:], f32)

    @pl.when(step + 1 < slots)
    def _():
        for c in fetch(step + 1, (step + 1) % 2) + mask_list(step + 1, (step + 1) % 2):
            c.start()

    @pl.when(step < slots)
    def _():
        block = step
        slot = block % 2
        for c in fetch(block, slot) + mask_list(block, slot):
            c.wait()
        left = lax.broadcasted_iota(jnp.int32, (1, 2 * length), 1) < length
        for pair in range(H // 2):
            cols = pl.ds(pair * 2 * HD, 2 * HD)
            vcols = pl.ds(width + pair * 2 * HD, 2 * HD)
            rows = pl.ds(pair * 2 * length, 2 * length)
            queries = split_heads(q_ref[0, :, cols])
            grads = split_heads(g_ref[0, :, cols])
            lse = lse_ref[0, :, rows]
            p_scr[...] = nt(buf[slot, :, cols], queries)
            g_scr[...] = nt(buf[slot, :, vcols], grads)
            inner = None
            for j in range(listed + 1):
                part = pl.ds(j * length, length)
                at = (block * H + pair * 2) * (listed + 1) + j
                row = jnp.where(left, bias_ref[at], bias_ref[at + listed + 1]) - lse
                mask = mcol[slot, part]
                mask = jnp.concatenate([mask, mask], 1)
                probs = jnp.exp(p_scr[part] + row + mask)
                p_scr[part] = probs
                pl_scr[part] = probs.astype(bf16)
                term = jnp.sum(probs * g_scr[part], axis=0, keepdims=True)
                inner = term if inner is None else inner + term
            for j in range(listed + 1):
                part = pl.ds(j * length, length)
                ds = p_scr[part] * (g_scr[part] - inner)
                ds_scr[part] = ds.astype(bf16)
                dbias_ref[0, pl.ds(j, 1), rows] = jnp.sum(ds, axis=0, keepdims=True)
            dq = tn(ds_scr[...], buf[slot, :, cols])
            dq_ref[0, :, cols] = (join_heads(dq) * scale).astype(bf16)
            dk = nn(ds_scr[...], queries)
            dv = nn(pl_scr[...], grads)
            down_ref[0, :, cols] = dk[:length].astype(bf16)
            down_ref[0, :, vcols] = dv[:length].astype(bf16)
            for j in range(listed):
                at = (j // 2) * slots + nbr_ref[block * listed + j]
                acc[at, :, cols] += dk[(j + 1) * length : (j + 2) * length]
                acc[at, :, vcols] += dv[(j + 1) * length : (j + 2) * length]

    @pl.when(step >= slots)
    def _():
        for o in range(4):
            dfar_ref[o, 0] = acc[o * slots + step - slots].astype(bf16)


def attend_back(nbr, bias, queries, grads, lse, mask_cols, own, far):
    slots, length, width = queries.shape
    listed = nbr.shape[0] // slots
    keys = (listed + 1) * length
    any_spec = pl.BlockSpec(memory_space=pl.ANY)
    here = lambda b, *_: (jnp.minimum(b, slots - 1), 0, 0)
    return pl.pallas_call(
        functools.partial(backward_body, listed, slots),
        grid_spec=pltpu.PrefetchScalarGridSpec(
            num_scalar_prefetch=2,
            grid=(2 * slots,),
            in_specs=[
                pl.BlockSpec((1, length, width), here),
                pl.BlockSpec((1, length, width), here),
                pl.BlockSpec((1, 1, H * length), here),
            ]
            + [any_spec] * 6,
            out_specs=[
                pl.BlockSpec((1, length, width), here),
                pl.BlockSpec((1, length, 2 * width), here),
                pl.BlockSpec(
                    (4, 1, length, 2 * width), lambda b, *_: (0, jnp.maximum(b - slots, 0), 0, 0)
                ),
                pl.BlockSpec((1, listed + 1, H * length), here),
            ],
            scratch_shapes=[
                pltpu.VMEM((2, keys, 2 * width), bf16),
                pltpu.VMEM((2, keys, length), f32),
                pltpu.VMEM((keys, 2 * length), f32),
                pltpu.VMEM((keys, 2 * length), f32),
                pltpu.VMEM((keys, 2 * length), bf16),
                pltpu.VMEM((keys, 2 * length), bf16),
                pltpu.VMEM((4 * slots, length, 2 * width), f32),
                pltpu.SemaphoreType.DMA((2, listed + 1)),
                pltpu.SemaphoreType.DMA((2, listed + 1)),
            ],
        ),
        out_shape=[
            jax.ShapeDtypeStruct((slots, length, width), bf16),
            jax.ShapeDtypeStruct((slots, length, 2 * width), bf16),
            jax.ShapeDtypeStruct((4, slots, length, 2 * width), bf16),
            jax.ShapeDtypeStruct((slots, listed + 1, H * length), f32),
        ],
        cost_estimate=pl.CostEstimate(
            flops=10 * slots * length * keys * width * 2,
            bytes_accessed=slots * keys * width * 4,
            transcendentals=slots * length * keys * H,
        ),
        compiler_params=pltpu.CompilerParams(vmem_limit_bytes=60 << 20),
        name="attention_backward",
    )(nbr, bias, queries, grads, lse, mask_cols, own, *far)


def halved(value, order):
    count = value.shape[0]
    bits = count.bit_length() - 1
    place = lax.axis_index(both)
    value = value.reshape((2,) * bits + value.shape[1:])
    left = list(range(bits - 1, -1, -1))
    for bit in order:
        axis = left.index(bit)
        left.pop(axis)
        mine = (place >> bit) & 1
        keep = lax.dynamic_index_in_dim(value, mine, axis, keepdims=False)
        send = lax.dynamic_index_in_dim(value, 1 - mine, axis, keepdims=False)
        got = lax.ppermute(send, both, [(i, i ^ (1 << bit)) for i in range(count)])
        value = keep + got
    return value


def bit_orders(count):
    bits = list(range(count.bit_length() - 1))
    rest = bits[1:]
    orders = []
    for turn in range(4):
        k = turn % len(rest)
        orders.append(bits[:1] + rest[k:] + rest[:k])
    return orders


def per_device(
    features,
    targets,
    node_mask,
    block_counts,
    neighbours,
    edge_types,
    proj_weights,
    ffn_weights,
    vector_params,
    proj_mean,
    ffn_mean,
    vector_mean,
    proj_square,
    ffn_square,
    vector_square,
):
    span_count = lax.axis_size("nodes")
    pair_count = lax.axis_size("fsdp")
    device_count = span_count * pair_count
    slot_count, listed = neighbours.shape
    row_count, model_width = features.shape
    block_len = row_count // slot_count
    shard = proj_weights.shape[1]
    shifts = (1, -1, span_count // 4, span_count // 2)

    far_features = [passed_along(features, s) for s in shifts]

    live_slots = (jnp.arange(slot_count) < block_counts[0]).astype(f32)
    valid_nodes = node_mask.astype(f32).reshape(slot_count, block_len) * live_slots[:, None]
    valid_rows = valid_nodes.reshape(row_count)

    mask_rows = row_count // model_width
    used_rows = 5 * shard + 1 + mask_rows
    packed = jnp.concatenate(
        [
            proj_weights.astype(bf16).reshape(5 * shard, model_width),
            jnp.pad(vector_params.astype(bf16).reshape(1, 8 * shard), ((0, 0), (0, model_width - 8 * shard))),
            valid_rows.astype(bf16).reshape(mask_rows, model_width),
            jnp.zeros((-used_rows % 16, model_width), bf16),
        ],
        0,
    )
    gathered = lax.all_gather(packed, both, axis=0, tiled=False)
    low_ffn = lax.all_gather(ffn_weights.astype(bf16), both, axis=1, tiled=True)
    low_proj = (
        gathered[:, : 5 * shard]
        .reshape(device_count, 5, shard, model_width)
        .transpose(1, 0, 2, 3)
        .reshape(5, model_width, model_width)
    )
    low_vector = (
        gathered[:, 5 * shard, : 8 * shard]
        .reshape(device_count, 8, shard)
        .transpose(1, 0, 2)
        .reshape(8, model_width)
    )
    all_valid = gathered[:, 5 * shard + 1 : used_rows].astype(f32)
    node_total = jnp.sum(all_valid)
    gain_rows = low_vector.astype(f32)

    rank = lax.axis_index("nodes")
    pair = lax.axis_index("fsdp")
    all_valid = all_valid.reshape(device_count, slot_count, block_len)
    far_valid = [
        lax.dynamic_index_in_dim(
            all_valid, ((rank - s) % span_count) * pair_count + pair, 0, keepdims=False
        )
        for s in shifts
    ]
    key_masks = (jnp.concatenate([valid_nodes] + far_valid, 0) - 1.0) * mask_fill
    mask_lines = key_masks[:, None, :]
    mask_cols = jnp.broadcast_to(key_masks[:, :, None], key_masks.shape + (block_len,))

    type_table = gain_rows[7].reshape(NTYPES, H)
    type_onehot = (
        edge_types[:, :, None] == jnp.arange(NTYPES, dtype=jnp.int32)[None, None, :]
    ).astype(f32)
    pair_bias = jnp.einsum("sjt,th->shj", type_onehot, type_table, precision=precise).reshape(-1)
    flat_nbr = neighbours.reshape(-1)

    base, attn_in, queries, own_kv = project(features, low_proj, gain_rows, True)
    far_a1 = []
    far_kv = []
    for piece in far_features:
        a1, kv = project(piece, low_proj, gain_rows, False)
        far_a1.append(a1)
        far_kv.append(kv.reshape(slot_count, block_len, 2 * model_width))
    own_blocks = own_kv.reshape(slot_count, block_len, 2 * model_width)
    query_blocks = queries.reshape(slot_count, block_len, model_width)

    attn_out, lse = attend(flat_nbr, pair_bias, query_blocks, mask_lines, own_blocks, far_kv)
    attn_rows = attn_out.reshape(row_count, model_width)
    attn_y = nn(attn_rows, low_proj[4])
    middle = base + attn_y
    normed_two, norm_two_back = jax.vjp(layer_norm, middle, gain_rows[2], gain_rows[3])
    ffn_in = normed_two.astype(bf16)
    hidden_pre = nn(ffn_in, low_ffn[0])
    hidden_act, gelu_back = jax.vjp(jax.nn.gelu, hidden_pre)
    hidden = hidden_act.astype(bf16)
    ffn_y = nt(hidden, low_ffn[1])
    final = middle + ffn_y
    predict, head_back = jax.vjp(head_out, final, gain_rows[4], gain_rows[5], gain_rows[6])
    error = predict - targets
    local_sums = jnp.stack(
        [jnp.sum(valid_rows * error * error)]
        + [jnp.sum(valid_rows[:, None] * piece * piece) for piece in (middle, attn_y, final, ffn_y)]
    )

    grad_pred = 2.0 * valid_rows * error / node_total
    grad_final, grad_gain_f, grad_shift_f, grad_head = head_back(grad_pred)
    grad_ffn_y = grad_final.astype(bf16)
    grad_down = tn(grad_ffn_y, hidden)
    grad_hidden = nn(grad_ffn_y, low_ffn[1])
    grad_pre = gelu_back(grad_hidden)[0].astype(bf16)
    grad_up = tn(ffn_in, grad_pre)
    shard_ffn = lax.psum_scatter(
        jnp.stack([grad_up, grad_down]), both, scatter_dimension=1, tiled=True
    )
    grad_ffn_in = nt(grad_pre, low_ffn[0])
    grad_mid_norm, grad_gain_two, grad_shift_two = norm_two_back(grad_ffn_in)
    grad_middle = grad_final + grad_mid_norm
    grad_attn_y = grad_middle.astype(bf16)
    grad_out_proj = tn(attn_rows, grad_attn_y)
    grad_attn = nt(grad_attn_y, low_proj[4]).astype(bf16).reshape(query_blocks.shape)

    grad_q, grad_own, grad_far, grad_bias = attend_back(
        flat_nbr, pair_bias, query_blocks, grad_attn, lse, mask_cols, own_blocks, far_kv
    )
    grad_q = grad_q.reshape(row_count, model_width)
    grad_own = grad_own.reshape(row_count, 2 * model_width)
    low_kv = jnp.concatenate([low_proj[2], low_proj[3]], 1)
    back_pieces = []
    for index, shift_by in reversed(list(enumerate(shifts))):
        piece = grad_far[index].reshape(row_count, 2 * model_width)
        back_pieces.append(passed_along(nt(piece, low_kv).astype(bf16), -shift_by))
    grad_query_w = tn(attn_in, grad_q)
    grad_kv_w = tn(attn_in, grad_own)
    for index in range(4):
        grad_kv_w = grad_kv_w + tn(far_a1[index], grad_far[index].reshape(row_count, 2 * model_width))
    early = jnp.stack(
        [grad_query_w, grad_kv_w[:, :model_width], grad_kv_w[:, model_width:], grad_out_proj]
    )
    early = early.reshape(4, device_count, shard, model_width)
    shard_early = [
        halved(early[index], order) for index, order in enumerate(bit_orders(device_count))
    ]
    grad_attn_in = nt(grad_q, low_proj[1]) + nt(grad_own, low_kv)
    for piece in back_pieces:
        grad_attn_in = grad_attn_in + piece.astype(f32)
    _, norm_one_back = jax.vjp(layer_norm, base, gain_rows[0], gain_rows[1])
    grad_base_norm, grad_gain_one, grad_shift_one = norm_one_back(grad_attn_in)
    grad_base = (grad_middle + grad_base_norm).astype(bf16)
    grad_encoder = tn(features, grad_base)
    bias_sums = jnp.sum(grad_bias.reshape(slot_count, listed + 1, H, block_len), -1)
    grad_table = jnp.einsum("sjt,sjh->th", type_onehot, bias_sums, precision=precise)
    grad_vector_all = jnp.stack(
        [
            grad_gain_one,
            grad_shift_one,
            grad_gain_two,
            grad_shift_two,
            grad_gain_f,
            grad_shift_f,
            grad_head,
            grad_table.reshape(model_width),
        ]
    )
    vector_lines = (
        grad_vector_all.reshape(8, device_count, shard)
        .transpose(1, 0, 2)
        .reshape(device_count, 1, 8 * shard)
    )
    vector_lines = jnp.pad(vector_lines, ((0, 0), (0, 0), (0, model_width - 8 * shard)))
    late = jnp.concatenate(
        [grad_encoder.reshape(device_count, shard, model_width), vector_lines], 1
    )
    late = halved(late, list(range(device_count.bit_length() - 1)))
    shard_proj = jnp.stack([late[:shard]] + shard_early)
    shard_vector = late[shard, : 8 * shard].reshape(8, shard)

    proj_parts = lamb_parts(proj_weights, shard_proj, proj_mean, proj_square, (1, 2))
    ffn_parts = lamb_parts(ffn_weights, shard_ffn, ffn_mean, ffn_square, (1, 2))
    vector_parts = lamb_parts(vector_params, shard_vector, vector_mean, vector_square, (1,))
    mine = jnp.concatenate(
        [
            proj_parts[3], ffn_parts[3], vector_parts[3],
            proj_parts[4], ffn_parts[4], vector_parts[4],
            local_sums,
        ]
    )
    mine = jnp.pad(mine, (0, 128 - mine.shape[0]))
    everyone = lax.all_to_all(
        jnp.broadcast_to(mine[None], (device_count, 128)), both, 0, 0, tiled=True
    )
    sums = jnp.sum(everyone, 0)
    norm_pairs = jnp.sqrt(jnp.stack([sums[:15], sums[15:30]], 1))
    stat_sums = sums[30:35]
    ratio = norm_pairs[:, 0] / norm_pairs[:, 1]
    updated_proj = proj_weights - learn_rate * ratio[0:5, None, None] * proj_parts[2]
    updated_ffn = ffn_weights - learn_rate * ratio[5:7, None, None] * ffn_parts[2]
    updated_vector = vector_params - learn_rate * ratio[7:15, None] * vector_parts[2]
    train_loss = stat_sums[0] / node_total
    stream_scale = jnp.sqrt(stat_sums[1:] / (node_total * model_width))
    return (
        updated_proj,
        updated_ffn,
        updated_vector,
        proj_parts[0],
        ffn_parts[0],
        vector_parts[0],
        proj_parts[1],
        ffn_parts[1],
        vector_parts[1],
        updated_proj.astype(bf16),
        updated_ffn.astype(bf16),
        updated_vector.astype(bf16),
        norm_pairs,
        stream_scale,
        train_loss,
    )


def solution(mesh):
    rows = P(("nodes", "fsdp"), None)
    line = P(("nodes", "fsdp"))
    cube = P(None, ("nodes", "fsdp"), None)
    flat = P(None, ("nodes", "fsdp"))
    state = (cube, cube, flat)
    return jax.shard_map(
        per_device,
        mesh=mesh,
        in_specs=(rows, line, line, line, rows, rows) + state * 3,
        out_specs=state * 4 + (P(), P(), P()),
        check_vma=False,
    )
```

time: 2150 us -> 790 us (0.37)
  waiting for transfers between devices: 857 us -> 324 us
  local copies, waits for them, and re-layouts: 412 us -> 76.7 us
  other arithmetic: 346 us -> 45.6 us
  matrix products: 275 us -> 91.4 us
  blocking collectives: 139 us -> 0 us
  Pallas kernels: 0 us -> 135 us
    reduce_scatter x2 -> x1, waiting for transfers between devices: 294 us -> 0.01 us  [per_device(): lax.psum_scatter(jnp.stack([grad_up, grad_down]), both, scatter_dimension...]
    ppermute x12 -> x33, waiting for transfers between devices: 394 us -> 159 us  [the longest x25 159 us: halved(): got = lax.ppermute(send, both, [(i, i ^ 1 << bit) for i in range(count)])]
    dot_general x36 -> x23, matrix products: 275 us -> 91.1 us  [the longest x9 41.1 us: nt(): lax.dot_general(a, b, (((1,), (1,)), ((), ())), preferred_element_type=f32)]
    unnamed x6 -> x3, waiting for transfers between devices: 141 us -> 0.05 us
    pallas_call x0 -> x7, Pallas kernels: none -> 135 us  [the longest x1 64.5 us: attend_back(): pl.pallas_call(functools.partial(backward_body, listed, slots), grid_spec...]
    all_gather x2, waiting for transfers between devices: 27.7 us -> 161 us  [the longest x1 161 us: per_device(): gathered = lax.all_gather(packed, both, axis=0, tiled=False)]
    psum x2 -> x0, blocking collectives: 108 us -> none  [the longest x1 62.7 us: per_device(): norm_squares = lax.psum(local_squares, ('nodes', 'fsdp'))]
    scatter-add x3 -> x0, other arithmetic: 107 us -> none  [backward_group(): grad_remote.at[flat_index]]
  transfers between devices with their start and end apart: 17 -> 37, of which waited for: 11 -> 13; matrix products, arithmetic and copies ran while one was open for 12% -> 17% of each run, Pallas kernels for 0% -> 17%
where the time goes in v1:
time: 790 us; the launch traced here: 777 us
  waiting for transfers between devices  324 us (41%)
  Pallas kernels  135 us (17%)
  matrix products  91.4 us (12%)
  starting transfers between devices  85.1 us (11%)
  local copies, waits for them, and re-layouts  76.7 us (10%)
  other arithmetic  45.6 us (6%)
  between operations  19.4 us (2%)
    all_gather x1, waiting for transfers between devices, per_device(): gathered = lax.all_gather(packed, both, axis=0, tiled=False)  161 us
    ppermute x25, waiting for transfers between devices, halved(): got = lax.ppermute(send, both, [(i, i ^ 1 << bit) for i in range(count)])  159 us
    ppermute x25, starting transfers between devices, halved(): got = lax.ppermute(send, both, [(i, i ^ 1 << bit) for i in range(count)])  69.9 us
    pallas_call x1, Pallas kernels, attend_back(): pl.pallas_call(functools.partial(backward_body, listed, slots), grid_spec...  64.5 us
    pallas_call x1, Pallas kernels, attend(): pl.pallas_call(functools.partial(forward_body, listed, slots), grid_spec=...  44.6 us
    dot_general x9, matrix products, nt(): lax.dot_general(a, b, (((1,), (1,)), ((), ())), preferred_element_type=f32)  41.1 us
    unnamed x176, local copies, waits for them, and re-layouts  27.3 us
    dot_general x3, matrix products, nn(): lax.dot_general(a, b, (((1,), (0,)), ((), ())), preferred_element_type=f32)  26.7 us
  transfers between devices with their start and end apart: 37, of which 13 were waited for; matrix products, arithmetic and copies ran while one was open for 17% of the time, Pallas kernels for 17%

profile of v1, /device:TPU:10, one launch (start us, length us, event | category | flops | bytes accessed | tf_op | source)
XLA Modules:
  0.0 776.9 jit_solution(8942002800705792039)
XLA Ops:
  20.3 160.6 %all-gather.6.cloned.1.call-done = bf16[3072,512]{1,0:T(8,128)(2,1)} async-done(((bf16[96,512]{1,0:T(8,128)(2,1)}), bf16[3072,512]{1,0:T(8,128)(2,1)}) %all-gather.6.cloned.1.call-update) | async-done | bytes 3145744 | tf_op jit(solution)/shard_map/all_gather | solution.py:474
  190.4 5.0 project_remote.4
  195.4 5.4 project_remote.5
  202.0 5.4 project_remote.6
  209.0 5.5 project_remote.7
  217.4 4.7 project_local.1
  224.8 44.6 %attention_forward.1 = (bf16[12,128,512]{2,1,0:T(8,128)(2,1)S(1)}, f32[12,1,1024]{2,1,0:T(1,128)S(1)}) custom-call(s32[96]{0:T(128)S(1)} %reshape.428.nbr_ref, f32[864]{0:T(1024)S(1)} %reshape.429.bias_ref, bf16[12,128,512]{2,1,0:T(8,128)(2,1)S(1)} %bitcast.283, f32[60,1,128]{2,1,0:T(1,128)S(1)} %add_multiply_fusion.1.mask_ref, ...), custom_call_target="tpu_custom_call" | custom-call | flops 7247757312 | bytes 28311552 | tf_op jit(solution)/shard_map/attention_forward/pallas_call | solution.py:226
  288.3 10.8 %fusion.16 = f32[1536,2048]{1,0:T(8,128)} fusion(bf16[2,512,2048]{2,1,0:T(8,128)(2,1)} %all-gather.4.cloned.1.call-done, f32[1536,512]{1,0:T(8,128)} %copy-done.28, f32[512]{0:T(512)S(1)} %add.390, f32[512]{0:T(512)S(1)} %mul.523, f32[1536]{0:T(1024)S(1)} %fusion.39, f32[1536]{0:T(1024)S(1)} %broadcast_multiply_fusion.2), kind=kOutput, calls=%fused_computation.58 | convolution fusion | flops 3225157632 | bytes 17842176 | tf_op jit(solution)/shard_map/dot_general | solution.py:63
  299.1 7.8 %fusion.53 = (f32[1536]{0:T(1024)S(1)}, f32[1536,512]{1,0:T(8,128)S(1)}, f32[1536,512]{1,0:T(8,128)S(1)}) fusion(f32[1536,512]{1,0:T(8,128)S(1)} %copy-done.29, bf16[2,512,2048]{2,1,0:T(8,128)(2,1)S(1)} %copy-done.74, f32[1536,2048]{1,0:T(8,128)} %fusion.16), kind=kOutput, calls=%fused_computation.234 | convolution fusion | flops 3251108352 | bytes 24123392 | tf_op jit(solution)/shard_map/dot_general | solution.py:67
  317.5 6.7 convolution_bitcast_fusion
  324.2 13.1 %fusion.6 = bf16[1536,2048]{1,0:T(8,128)(2,1)S(1)} fusion(f32[1536,2048]{1,0:T(8,128)} %fusion.16, bf16[2,512,2048]{2,1,0:T(8,128)(2,1)S(1)} %copy-done.74, f32[1536]{0:T(1024)S(1)} %negate_multiply_fusion.2, f32[1536,512]{1,0:T(8,128)S(1)} %get-tuple-element.92, f32[1536]{0:T(1024)S(1)} %multiply_multiply_fusion.13, f32[1536]{0:T(1024)S(1)} %get-tuple-element.135, ...), kind=kOutput, calls=%fused_computation.8 | convolution fusion | flops 3291217920 | bytes 24162304 | tf_op jit(solution)/shard_map/dot_general | solution.py:63
  345.7 9.0 %multiply_reduce_fusion.2 = (f32[512]{0:T(512)S(1)}, f32[1536]{0:T(1024)S(1)}, f32[]{:T(128)}, f32[512]{0:T(512)S(1)}, f32[1536,512]{1,0:T(8,128)S(1)}) fusion(f32[1536,512]{1,0:T(8,128)} %copy-done.28, f32[1536]{0:T(1024)S(1)} %fusion.39, f32[1536]{0:T(1024)S(1)} %broadcast_multiply_fusion.2, f32[512]{0:T(512)S(1)} %mul.523, ...), kind=kOutput, calls=%fused_computation.33 | convolution fusion | flops 3229873664 | bytes 14710788 | tf_op jit(solution)/shard_map/dot_general | solution.py:67
  365.4 64.5 %attention_backward.1 = (bf16[12,128,512]{2,1,0:T(8,128)(2,1)}, bf16[12,128,1024]{2,1,0:T(8,128)(2,1)}, bf16[4,12,128,1024]{3,2,1,0:T(8,128)(2,1)}, f32[12,9,1024]{2,1,0:T(8,128)}) custom-call(s32[96]{0:T(128)} %copy-done.12, f32[864]{0:T(1024)} %copy-done.11, bf16[12,128,512]{2,1,0:T(8,128)(2,1)} %bitcast.284, bf16[12,128,512]{2,1,0:T(8,128)(2,1)} %bitcast.309, ...), custom_call_target="tpu_custom_call" | custom-call | flops 18119393280 | bytes 28311552 | tf_op jit(solution)/shard_map/attention_backward/pallas_call | solution.py:357
  429.9 6.1 fusion.56
  483.8 65.1 %collective-permute-done.24 = f32[2,2,2,16,512]{4,3,2,1,0:T(8,128)S(1)} collective-permute-done((f32[2,2,2,16,512]{4,3,2,1,0:T(8,128)S(1)}, f32[2,2,2,16,512]{4,3,2,1,0:T(8,128)S(1)}, u32[]{:S(2)}, u32[]{:S(2)}) %collective-permute-start.24) | collective-permute-done | bytes 262176 | tf_op jit(solution)/shard_map/ppermute | solution.py:416
  548.9 39.2 %collective-permute-start.19 = (f32[2,2,2,16,512]{4,3,2,1,0:T(8,128)S(1)}, f32[2,2,2,16,512]{4,3,2,1,0:T(8,128)S(1)}, u32[]{:S(2)}, u32[]{:S(2)}) collective-permute-start(f32[2,2,2,16,512]{4,3,2,1,0:T(8,128)S(1)} %dynamic-slice_bitcast_fusion.4), channel_id=1, source_target_pairs={{0,4},{1,5},{2,6},{3,7},{4,0},{5,1},{6,2},{7,3},{8,12},{9,13},{10,... | collective-permute-start | bytes 786440 | tf_op jit(solution)/shard_map/ppermute | solution.py:416
  589.5 38.4 %collective-permute-done.19 = f32[2,2,2,16,512]{4,3,2,1,0:T(8,128)S(1)} collective-permute-done((f32[2,2,2,16,512]{4,3,2,1,0:T(8,128)S(1)}, f32[2,2,2,16,512]{4,3,2,1,0:T(8,128)S(1)}, u32[]{:S(2)}, u32[]{:S(2)}) %collective-permute-start.19) | collective-permute-done | bytes 262176 | tf_op jit(solution)/shard_map/ppermute | solution.py:416
  628.0 30.1 %collective-permute-done.14 = f32[2,2,2,16,512]{4,3,1,0,2:T(8,128)S(1)} collective-permute-done((f32[2,2,2,16,512]{4,3,1,0,2:T(8,128)S(1)}, f32[2,2,2,16,512]{4,3,1,0,2:T(8,128)S(1)}, u32[]{:S(2)}, u32[]{:S(2)}) %collective-permute-start.14) | collective-permute-done | bytes 262176 | tf_op jit(solution)/shard_map/ppermute | solution.py:416
  658.8 4.7 collective-permute-done.30
  663.5 5.2 collective-permute-start.25
  671.6 8.4 %collective-permute-start.20 = (f32[2,2,16,512]{3,2,1,0:T(8,128)S(1)}, f32[2,2,16,512]{3,2,1,0:T(8,128)S(1)}, u32[]{:S(2)}, u32[]{:S(2)}) collective-permute-start(f32[2,2,16,512]{3,2,1,0:T(8,128)S(1)} %dynamic-slice_bitcast_fusion.7), channel_id=1, source_target_pairs={{0,8},{1,9},{2,10},{3,11},{4,12},{5,13},{6,14},{7,15},{8,0},{9,1},... | collective-permute-start | bytes 393224 | tf_op jit(solution)/shard_map/ppermute | solution.py:416
  686.2 6.2 multiply_reduce_fusion.3
  723.3 6.2 collective-permute-done.9
  753.6 5.2 all-to-all-start
  (422 shorter events, 199.7 us)
Async XLA Ops:
  7.2 173.8 %all-gather.6.cloned.1.call-start = ((), (), s32[]{:S(2)}) async-start(), calls=%async_computation.4 | async-start | bytes 3244032 | tf_op jit(solution)/shard_map/all_gather | solution.py:474
  11.2 277.1 %all-gather.4.cloned.1.call-start = ((), (), s32[]{:S(2)}) async-start(), calls=%async_computation.2 | async-start | bytes 4325376 | tf_op jit(solution)/shard_map/all_gather | solution.py:475
  12.9 735.3 %reduce-scatter.2.cloned.1.call-start = ((), (), s32[]{:S(2)}) async-start(), calls=%async_computation.3 | async-start | bytes 8650752 | tf_op jit(solution)/shard_map/reduce_scatter | solution.py:547
  13.0 177.4 %collective-permute-start = (bf16[1536,512]{1,0:T(8,128)(2,1)}, bf16[1536,512]{1,0:T(8,128)(2,1)}, u32[]{:S(2)}, u32[]{:S(2)}) collective-permute-start(bf16[1536,512]{1,0:T(8,128)(2,1)} %x_ref.1), channel_id=1, source_target_pairs={{0,2},{2,4},{4,6},{6,8},{8,10},{10,12},{12,14},{14,16},{16,18},{18... | collective-permute-start | bytes 4718600 | tf_op jit(solution)/shard_map/ppermute | solution.py:31
  14.5 180.9 %collective-permute-start.1 = (bf16[1536,512]{1,0:T(8,128)(2,1)}, bf16[1536,512]{1,0:T(8,128)(2,1)}, u32[]{:S(2)}, u32[]{:S(2)}) collective-permute-start(bf16[1536,512]{1,0:T(8,128)(2,1)} %x_ref.1), channel_id=1, source_target_pairs={{0,30},{2,0},{4,2},{6,4},{8,6},{10,8},{12,10},{14,12},{16,14},{18,... | collective-permute-start | bytes 4718600 | tf_op jit(solution)/shard_map/ppermute | solution.py:31
  15.0 186.9 %collective-permute-start.2 = (bf16[1536,512]{1,0:T(8,128)(2,1)}, bf16[1536,512]{1,0:T(8,128)(2,1)}, u32[]{:S(2)}, u32[]{:S(2)}) collective-permute-start(bf16[1536,512]{1,0:T(8,128)(2,1)} %x_ref.1), channel_id=1, source_target_pairs={{0,8},{2,10},{4,12},{6,14},{8,16},{10,18},{12,20},{14,22},{16,24},... | collective-permute-start | bytes 4718600 | tf_op jit(solution)/shard_map/ppermute | solution.py:31
  16.6 192.3 %collective-permute-start.3 = (bf16[1536,512]{1,0:T(8,128)(2,1)}, bf16[1536,512]{1,0:T(8,128)(2,1)}, u32[]{:S(2)}, u32[]{:S(2)}) collective-permute-start(bf16[1536,512]{1,0:T(8,128)(2,1)} %x_ref.1), channel_id=1, source_target_pairs={{0,16},{2,18},{4,20},{6,22},{8,24},{10,26},{12,28},{14,30},{16,0},... | collective-permute-start | bytes 4718600 | tf_op jit(solution)/shard_map/ppermute | solution.py:31
  362.5 111.2 %collective-permute-start.28 = (f32[2,2,2,2,16,512]{5,4,3,2,1,0:T(8,128)}, f32[2,2,2,2,16,512]{5,4,3,2,1,0:T(8,128)}, u32[]{:S(2)}, u32[]{:S(2)}) collective-permute-start(f32[2,2,2,2,16,512]{5,4,3,2,1,0:T(8,128)} %dynamic-slice_bitcast_fusion), channel_id=1, source_target_pairs={{0,1},{1,0},{2,3},{3,2},{4,5},{5,4},{6,7},{7,6},{8,9},{9,8},{10,11... | collective-permute-start | bytes 1572872 | tf_op jit(solution)/shard_map/ppermute | solution.py:416
  446.8 28.3 %collective-permute-start.23 = (f32[2,2,2,2,16,512]{5,4,3,2,0,1:T(8,128)}, f32[2,2,2,2,16,512]{5,4,3,2,0,1:T(8,128)}, u32[]{:S(2)}, u32[]{:S(2)}) collective-permute-start(f32[2,2,2,2,16,512]{5,4,3,2,0,1:T(8,128)} %bitcast.246), channel_id=1, source_target_pairs={{0,1},{1,0},{2,3},{3,2},{4,5},{5,4},{6,7},{7,6},{8,9},{9,8},{10,11... | collective-permute-start | bytes 1572872 | tf_op jit(solution)/shard_map/ppermute | solution.py:416
  447.6 30.3 %collective-permute-start.18 = (f32[2,2,2,2,16,512]{5,4,3,1,0,2:T(8,128)}, f32[2,2,2,2,16,512]{5,4,3,1,0,2:T(8,128)}, u32[]{:S(2)}, u32[]{:S(2)}) collective-permute-start(f32[2,2,2,2,16,512]{5,4,3,1,0,2:T(8,128)} %bitcast.247), channel_id=1, source_target_pairs={{0,1},{1,0},{2,3},{3,2},{4,5},{5,4},{6,7},{7,6},{8,9},{9,8},{10,11... | collective-permute-start | bytes 1572872 | tf_op jit(solution)/shard_map/ppermute | solution.py:416
  466.9 216.7 %collective-permute-start.4 = (bf16[1536,512]{1,0:T(8,128)(2,1)}, bf16[1536,512]{1,0:T(8,128)(2,1)}, u32[]{:S(2)}, u32[]{:S(2)}) collective-permute-start(bf16[1536,512]{1,0:T(8,128)(2,1)} %convolution_convert_fusion.4), channel_id=1, source_target_pairs={{0,16},{2,18},{4,20},{6,22},{8,24},{10,26},{12,28},{14,30},{16,0},... | collective-permute-start | bytes 4718600 | tf_op jit(solution)/shard_map/ppermute | solution.py:31
  473.7 211.9 %collective-permute-start.5 = (bf16[1536,512]{1,0:T(8,128)(2,1)}, bf16[1536,512]{1,0:T(8,128)(2,1)S(1)}, u32[]{:S(2)}, u32[]{:S(2)}) collective-permute-start(bf16[1536,512]{1,0:T(8,128)(2,1)} %convolution_convert_fusion.3), channel_id=1, source_target_pairs={{0,24},{2,26},{4,28},{6,30},{8,0},{10,2},{12,4},{14,6},{16,8},{18,... | collective-permute-start | bytes 4718600 | tf_op jit(solution)/shard_map/ppermute | solution.py:31
  475.3 210.7 %collective-permute-start.6 = (bf16[1536,512]{1,0:T(8,128)(2,1)S(1)}, bf16[1536,512]{1,0:T(8,128)(2,1)S(1)}, u32[]{:S(2)}, u32[]{:S(2)}) collective-permute-start(bf16[1536,512]{1,0:T(8,128)(2,1)S(1)} %copy-done.76), channel_id=1, source_target_pairs={{0,2},{2,4},{4,6},{6,8},{8,10},{10,12},{12,14},{14,16},{16,18},{18... | collective-permute-start | bytes 4718600 | tf_op jit(solution)/shard_map/ppermute | solution.py:31
  478.0 110.2 %collective-permute-start.29 = (f32[2,2,2,16,512]{4,3,1,0,2:T(8,128)S(1)}, f32[2,2,2,16,512]{4,3,1,0,2:T(8,128)S(1)}, u32[]{:S(2)}, u32[]{:S(2)}) collective-permute-start(f32[2,2,2,16,512]{4,3,1,0,2:T(8,128)S(1)} %bitcast.327), channel_id=1, source_target_pairs={{0,16},{1,17},{2,18},{3,19},{4,20},{5,21},{6,22},{7,23},{8,24},{9,... | collective-permute-start | bytes 786440 | tf_op jit(solution)/shard_map/ppermute | solution.py:416
  481.1 67.8 %collective-permute-start.24 = (f32[2,2,2,16,512]{4,3,2,1,0:T(8,128)S(1)}, f32[2,2,2,16,512]{4,3,2,1,0:T(8,128)S(1)}, u32[]{:S(2)}, u32[]{:S(2)}) collective-permute-start(f32[2,2,2,16,512]{4,3,2,1,0:T(8,128)S(1)} %dynamic-slice_bitcast_fusion.3), channel_id=1, source_target_pairs={{0,8},{1,9},{2,10},{3,11},{4,12},{5,13},{6,14},{7,15},{8,0},{9,1},... | collective-permute-start | bytes 786440 | tf_op jit(solution)/shard_map/ppermute | solution.py:416
  548.9 79.0 %collective-permute-start.19 = (f32[2,2,2,16,512]{4,3,2,1,0:T(8,128)S(1)}, f32[2,2,2,16,512]{4,3,2,1,0:T(8,128)S(1)}, u32[]{:S(2)}, u32[]{:S(2)}) collective-permute-start(f32[2,2,2,16,512]{4,3,2,1,0:T(8,128)S(1)} %dynamic-slice_bitcast_fusion.4), channel_id=1, source_target_pairs={{0,4},{1,5},{2,6},{3,7},{4,0},{5,1},{6,2},{7,3},{8,12},{9,13},{10,... | collective-permute-start | bytes 786440 | tf_op jit(solution)/shard_map/ppermute | solution.py:416
  588.2 97.9 %collective-permute-start.7 = (bf16[1536,512]{1,0:T(8,128)(2,1)S(1)}, bf16[1536,512]{1,0:T(8,128)(2,1)S(1)}, u32[]{:S(2)}, u32[]{:S(2)}) collective-permute-start(bf16[1536,512]{1,0:T(8,128)(2,1)S(1)} %copy-done.75), channel_id=1, source_target_pairs={{0,30},{2,0},{4,2},{6,4},{8,6},{10,8},{12,10},{14,12},{16,14},{18,... | collective-permute-start | bytes 4718600 | tf_op jit(solution)/shard_map/ppermute | solution.py:31
  627.9 30.2 %collective-permute-start.14 = (f32[2,2,2,16,512]{4,3,1,0,2:T(8,128)S(1)}, f32[2,2,2,16,512]{4,3,1,0,2:T(8,128)S(1)}, u32[]{:S(2)}, u32[]{:S(2)}) collective-permute-start(f32[2,2,2,16,512]{4,3,1,0,2:T(8,128)S(1)} %bitcast.328), channel_id=1, source_target_pairs={{0,2},{1,3},{2,0},{3,1},{4,6},{5,7},{6,4},{7,5},{8,10},{9,11},{10,... | collective-permute-start | bytes 786440 | tf_op jit(solution)/shard_map/ppermute | solution.py:416
  683.0 32.9 %collective-permute-start.15 = (f32[2,2,16,512]{3,2,1,0:T(8,128)}, f32[2,2,16,512]{3,2,1,0:T(8,128)}, u32[]{:S(2)}, u32[]{:S(2)}) collective-permute-start(f32[2,2,16,512]{3,2,1,0:T(8,128)} %dynamic-slice_bitcast_fusion.8), channel_id=1, source_target_pairs={{0,4},{1,5},{2,6},{3,7},{4,0},{5,1},{6,2},{7,3},{8,12},{9,13},{10,... | collective-permute-start | bytes 393224 | tf_op jit(solution)/shard_map/ppermute | solution.py:416
  683.6 35.3 %collective-permute-start.31 = (f32[2,16,512]{2,1,0:T(8,128)}, f32[2,16,512]{2,1,0:T(8,128)}, u32[]{:S(2)}, u32[]{:S(2)}) collective-permute-start(f32[2,16,512]{2,1,0:T(8,128)} %dynamic-slice_bitcast_fusion.9), channel_id=1, source_target_pairs={{0,4},{1,5},{2,6},{3,7},{4,0},{5,1},{6,2},{7,3},{8,12},{9,13},{10,... | collective-permute-start | bytes 196616 | tf_op jit(solution)/shard_map/ppermute | solution.py:416
  685.7 36.6 %collective-permute-start.26 = (f32[2,16,512]{2,1,0:T(8,128)}, f32[2,16,512]{2,1,0:T(8,128)}, u32[]{:S(2)}, u32[]{:S(2)}) collective-permute-start(f32[2,16,512]{2,1,0:T(8,128)} %dynamic-slice_bitcast_fusion.10), channel_id=1, source_target_pairs={{0,2},{1,3},{2,0},{3,1},{4,6},{5,7},{6,4},{7,5},{8,10},{9,11},{10,... | collective-permute-start | bytes 196616 | tf_op jit(solution)/shard_map/ppermute | solution.py:416
  686.0 44.1 %collective-permute-start.21 = (f32[2,16,512]{2,1,0:T(8,128)}, f32[2,16,512]{2,1,0:T(8,128)}, u32[]{:S(2)}, u32[]{:S(2)}) collective-permute-start(f32[2,16,512]{2,1,0:T(8,128)} %dynamic-slice_bitcast_fusion.11), channel_id=1, source_target_pairs={{0,16},{1,17},{2,18},{3,19},{4,20},{5,21},{6,22},{7,23},{8,24},{9,... | collective-permute-start | bytes 196616 | tf_op jit(solution)/shard_map/ppermute | solution.py:416
  719.8 28.1 %collective-permute-start.32 = (f32[16,512]{1,0:T(8,128)S(1)}, f32[16,512]{1,0:T(8,128)S(1)}, u32[]{:S(2)}, u32[]{:S(2)}) collective-permute-start(f32[16,512]{1,0:T(8,128)S(1)} %dynamic-slice_bitcast_fusion.13), channel_id=1, source_target_pairs={{0,8},{1,9},{2,10},{3,11},{4,12},{5,13},{6,14},{7,15},{8,0},{9,1},... | collective-permute-start | bytes 98312 | tf_op jit(solution)/shard_map/ppermute | solution.py:416
  723.2 24.5 %collective-permute-start.27 = (f32[16,512]{1,0:T(8,128)S(1)}, f32[16,512]{1,0:T(8,128)S(1)}, u32[]{:S(2)}, u32[]{:S(2)}) collective-permute-start(f32[16,512]{1,0:T(8,128)S(1)} %dynamic-slice_bitcast_fusion.14), channel_id=1, source_target_pairs={{0,4},{1,5},{2,6},{3,7},{4,0},{5,1},{6,2},{7,3},{8,12},{9,13},{10,... | collective-permute-start | bytes 98312 | tf_op jit(solution)/shard_map/ppermute | solution.py:416
  (93 other events, 2806.0 us)
Sparse Core Ops, SparseCore 0:
  11.4 169.4 all-gather.5
  184.4 61.3 all-gather.3
  345.8 126.4 reduce-scatter.1

commit v2 on v1

--- a/solution.py
+++ b/solution.py
@@ -163,7 +163,6 @@
     block = pl.program_id(0)
     length = q_ref.shape[1]
     width = q_ref.shape[2]
-    keys = (listed + 1) * length
     far = (r0, r1, r2, r3)
     fetch = functools.partial(
         fetch_list, nbr_ref=nbr_ref, own_ref=own_ref, far_refs=far, buf=buf, sems=sems,
@@ -258,51 +257,54 @@
     )(nbr, bias, queries, masks, own, *far)
 
 
-def backward_body(listed, slots, nbr_ref, bias_ref, q_ref, g_ref, lse_ref, mask_ref, own_ref,
-                  r0, r1, r2, r3, dq_ref, down_ref, dfar_ref, dbias_ref,
-                  buf, mcol, p_scr, g_scr, pl_scr, ds_scr, acc, sems, msems):
+def backward_body(listed, slots, own, first, count, nbr_ref, bias_ref, q_ref, g_ref, lse_ref,
+                  inner_ref, mask_ref, *refs):
+    refs = list(refs)
+    own_ref = refs.pop(0) if own else None
+    prev_ref = refs.pop(0) if own else None
+    far = [refs.pop(0) for _ in range(count // 2)]
+    dq_ref = refs.pop(0)
+    down_ref = refs.pop(0) if own else None
+    dfar_ref, dbias_ref, buf, mcol, p_scr, g_scr, pl_scr, ds_scr, acc, sems, msems = refs
     step = pl.program_id(0)
     length = q_ref.shape[1]
     width = q_ref.shape[2]
-    far = (r0, r1, r2, r3)
-    fetch = functools.partial(
-        fetch_list, nbr_ref=nbr_ref, own_ref=own_ref, far_refs=far, buf=buf, sems=sems,
-        listed=listed, length=length,
-    )
-
-    def mask_list(block, slot):
-        out = [
-            pltpu.make_async_copy(
-                mask_ref.at[block], mcol.at[slot, pl.ds(0, length)], msems.at[slot, 0]
-            )
-        ]
-        for j in range(listed):
+    lead = 1 if own else 0
+    blocks = count + lead
+
+    def fetch(block, slot):
+        out = []
+        for i in range(blocks):
+            part = pl.ds(i * length, length)
+            if i < lead:
+                source, mask_at = own_ref.at[block], block
+            else:
+                j = first + i - lead
+                at = nbr_ref[block * listed + j]
+                source, mask_at = far[(i - lead) // 2].at[at], (j // 2 + 1) * slots + at
+            out.append(pltpu.make_async_copy(source, buf.at[slot, part], sems.at[slot, i]))
             out.append(
-                pltpu.make_async_copy(
-                    mask_ref.at[(j // 2 + 1) * slots + nbr_ref[block * listed + j]],
-                    mcol.at[slot, pl.ds((j + 1) * length, length)],
-                    msems.at[slot, j + 1],
-                )
+                pltpu.make_async_copy(mask_ref.at[mask_at], mcol.at[slot, part], msems.at[slot, i])
             )
         return out
 
     @pl.when(step == 0)
     def _():
-        for c in fetch(0, 0) + mask_list(0, 0):
+        for c in fetch(0, 0):
             c.start()
-        for i in range(4 * slots):
+        for i in range(acc.shape[0]):
             acc[i] = jnp.zeros(acc.shape[1:], f32)
 
     @pl.when(step + 1 < slots)
     def _():
-        for c in fetch(step + 1, (step + 1) % 2) + mask_list(step + 1, (step + 1) % 2):
+        for c in fetch(step + 1, (step + 1) % 2):
             c.start()
 
     @pl.when(step < slots)
     def _():
         block = step
         slot = block % 2
-        for c in fetch(block, slot) + mask_list(block, slot):
+        for c in fetch(block, slot):
             c.wait()
         left = lax.broadcasted_iota(jnp.int32, (1, 2 * length), 1) < length
         for pair in range(H // 2):
@@ -312,67 +314,77 @@
             queries = split_heads(q_ref[0, :, cols])
             grads = split_heads(g_ref[0, :, cols])
             lse = lse_ref[0, :, rows]
+            inner = inner_ref[0, :, rows]
             p_scr[...] = nt(buf[slot, :, cols], queries)
             g_scr[...] = nt(buf[slot, :, vcols], grads)
-            inner = None
-            for j in range(listed + 1):
-                part = pl.ds(j * length, length)
+            for i in range(blocks):
+                part = pl.ds(i * length, length)
+                j = i if own else first + 1 + i
                 at = (block * H + pair * 2) * (listed + 1) + j
                 row = jnp.where(left, bias_ref[at], bias_ref[at + listed + 1]) - lse
                 mask = mcol[slot, part]
                 mask = jnp.concatenate([mask, mask], 1)
                 probs = jnp.exp(p_scr[part] + row + mask)
-                p_scr[part] = probs
                 pl_scr[part] = probs.astype(bf16)
-                term = jnp.sum(probs * g_scr[part], axis=0, keepdims=True)
-                inner = term if inner is None else inner + term
-            for j in range(listed + 1):
-                part = pl.ds(j * length, length)
-                ds = p_scr[part] * (g_scr[part] - inner)
+                ds = probs * (g_scr[part] - inner)
                 ds_scr[part] = ds.astype(bf16)
-                dbias_ref[0, pl.ds(j, 1), rows] = jnp.sum(ds, axis=0, keepdims=True)
-            dq = tn(ds_scr[...], buf[slot, :, cols])
-            dq_ref[0, :, cols] = (join_heads(dq) * scale).astype(bf16)
+                dbias_ref[0, pl.ds(i, 1), rows] = jnp.sum(ds, axis=0, keepdims=True)
+            dq = join_heads(tn(ds_scr[...], buf[slot, :, cols])) * scale
+            if own:
+                dq_ref[0, :, cols] = (dq + prev_ref[0, :, cols]).astype(bf16)
+            else:
+                dq_ref[0, :, cols] = dq
             dk = nn(ds_scr[...], queries)
             dv = nn(pl_scr[...], grads)
-            down_ref[0, :, cols] = dk[:length].astype(bf16)
-            down_ref[0, :, vcols] = dv[:length].astype(bf16)
-            for j in range(listed):
-                at = (j // 2) * slots + nbr_ref[block * listed + j]
-                acc[at, :, cols] += dk[(j + 1) * length : (j + 2) * length]
-                acc[at, :, vcols] += dv[(j + 1) * length : (j + 2) * length]
+            if own:
+                down_ref[0, :, cols] = dk[:length].astype(bf16)
+                down_ref[0, :, vcols] = dv[:length].astype(bf16)
+            for i in range(count):
+                part = slice((i + lead) * length, (i + lead + 1) * length)
+                at = (i // 2) * slots + nbr_ref[block * listed + first + i]
+                acc[at, :, cols] += dk[part]
+                acc[at, :, vcols] += dv[part]
 
     @pl.when(step >= slots)
     def _():
-        for o in range(4):
+        for o in range(count // 2):
             dfar_ref[o, 0] = acc[o * slots + step - slots].astype(bf16)
 
 
-def attend_back(nbr, bias, queries, grads, lse, mask_cols, own, far):
+def attend_back(nbr, bias, queries, grads, lse, inner, mask_cols, own, before, far, first):
     slots, length, width = queries.shape
     listed = nbr.shape[0] // slots
-    keys = (listed + 1) * length
+    lead = 0 if own is None else 1
+    count = 2 * len(far)
+    keys = (count + lead) * length
     any_spec = pl.BlockSpec(memory_space=pl.ANY)
     here = lambda b, *_: (jnp.minimum(b, slots - 1), 0, 0)
+    block_spec = pl.BlockSpec((1, length, width), here)
+    line_spec = pl.BlockSpec((1, 1, H * length), here)
+    outs = [jax.ShapeDtypeStruct((slots, length, width), bf16 if lead else f32)]
+    out_specs = [block_spec]
+    if lead:
+        outs.append(jax.ShapeDtypeStruct((slots, length, 2 * width), bf16))
+        out_specs.append(pl.BlockSpec((1, length, 2 * width), here))
+    outs += [
+        jax.ShapeDtypeStruct((len(far), slots, length, 2 * width), bf16),
+        jax.ShapeDtypeStruct((slots, count + lead, H * length), f32),
+    ]
+    out_specs += [
+        pl.BlockSpec(
+            (len(far), 1, length, 2 * width), lambda b, *_: (0, jnp.maximum(b - slots, 0), 0, 0)
+        ),
+        pl.BlockSpec((1, count + lead, H * length), here),
+    ]
     return pl.pallas_call(
-        functools.partial(backward_body, listed, slots),
+        functools.partial(backward_body, listed, slots, bool(lead), first, count),
         grid_spec=pltpu.PrefetchScalarGridSpec(
             num_scalar_prefetch=2,
             grid=(2 * slots,),
-            in_specs=[
-                pl.BlockSpec((1, length, width), here),
-                pl.BlockSpec((1, length, width), here),
-                pl.BlockSpec((1, 1, H * length), here),
-            ]
-            + [any_spec] * 6,
-            out_specs=[
-                pl.BlockSpec((1, length, width), here),
-                pl.BlockSpec((1, length, 2 * width), here),
-                pl.BlockSpec(
-                    (4, 1, length, 2 * width), lambda b, *_: (0, jnp.maximum(b - slots, 0), 0, 0)
-                ),
-                pl.BlockSpec((1, listed + 1, H * length), here),
-            ],
+            in_specs=[block_spec, block_spec, line_spec, line_spec, any_spec]
+            + [any_spec, block_spec] * lead
+            + [any_spec] * len(far),
+            out_specs=out_specs,
             scratch_shapes=[
                 pltpu.VMEM((2, keys, 2 * width), bf16),
                 pltpu.VMEM((2, keys, length), f32),
@@ -380,30 +392,29 @@
                 pltpu.VMEM((keys, 2 * length), f32),
                 pltpu.VMEM((keys, 2 * length), bf16),
                 pltpu.VMEM((keys, 2 * length), bf16),
-                pltpu.VMEM((4 * slots, length, 2 * width), f32),
-                pltpu.SemaphoreType.DMA((2, listed + 1)),
-                pltpu.SemaphoreType.DMA((2, listed + 1)),
+                pltpu.VMEM((len(far) * slots, length, 2 * width), f32),
+                pltpu.SemaphoreType.DMA((2, count + lead)),
+                pltpu.SemaphoreType.DMA((2, count + lead)),
             ],
         ),
-        out_shape=[
-            jax.ShapeDtypeStruct((slots, length, width), bf16),
-            jax.ShapeDtypeStruct((slots, length, 2 * width), bf16),
-            jax.ShapeDtypeStruct((4, slots, length, 2 * width), bf16),
-            jax.ShapeDtypeStruct((slots, listed + 1, H * length), f32),
-        ],
+        out_shape=outs,
         cost_estimate=pl.CostEstimate(
-            flops=10 * slots * length * keys * width * 2,
+            flops=20 * slots * length * keys * width * 2,
             bytes_accessed=slots * keys * width * 4,
             transcendentals=slots * length * keys * H,
         ),
-        compiler_params=pltpu.CompilerParams(vmem_limit_bytes=60 << 20),
-        name="attention_backward",
-    )(nbr, bias, queries, grads, lse, mask_cols, own, *far)
+        compiler_params=pltpu.CompilerParams(vmem_limit_bytes=48 << 20),
+        name="attention_backward_near" if lead else "attention_backward_far",
+    )(nbr, bias, queries, grads, lse, inner, mask_cols, *([own, before] if lead else []), *far)
+
+
+def swap(value, bit):
+    count = lax.axis_size("nodes") * lax.axis_size("fsdp")
+    return lax.ppermute(value, both, [(i, i ^ (1 << bit)) for i in range(count)])
 
 
 def halved(value, order):
-    count = value.shape[0]
-    bits = count.bit_length() - 1
+    bits = value.shape[0].bit_length() - 1
     place = lax.axis_index(both)
     value = value.reshape((2,) * bits + value.shape[1:])
     left = list(range(bits - 1, -1, -1))
@@ -413,19 +424,25 @@
         mine = (place >> bit) & 1
         keep = lax.dynamic_index_in_dim(value, mine, axis, keepdims=False)
         send = lax.dynamic_index_in_dim(value, 1 - mine, axis, keepdims=False)
-        got = lax.ppermute(send, both, [(i, i ^ (1 << bit)) for i in range(count)])
+        got = swap(send, bit)
         value = keep + got
     return value
 
 
-def bit_orders(count):
-    bits = list(range(count.bit_length() - 1))
-    rest = bits[1:]
-    orders = []
-    for turn in range(4):
-        k = turn % len(rest)
-        orders.append(bits[:1] + rest[k:] + rest[:k])
-    return orders
+def doubled(value, bits):
+    place = lax.axis_index(both)
+    for turn, bit in enumerate(range(bits - 1, -1, -1)):
+        got = swap(value, bit)
+        mine = (place >> bit) & 1
+        value = jnp.where(
+            mine == 0, jnp.stack([value, got], turn), jnp.stack([got, value], turn)
+        )
+    return value.reshape((1 << bits,) + value.shape[bits:])
+
+
+def orders_of(bits):
+    rest = list(range(3, bits))
+    return ([0, 1, 2] + rest, [0, 2, 1] + rest)
 
 
 def per_device(
@@ -454,7 +471,10 @@
     shard = proj_weights.shape[1]
     shifts = (1, -1, span_count // 4, span_count // 2)
 
-    far_features = [passed_along(features, s) for s in shifts]
+    bits = device_count.bit_length() - 1
+    far_features = [None] * 4
+    for index in (3, 2):
+        far_features[index] = passed_along(features, shifts[index])
 
     live_slots = (jnp.arange(slot_count) < block_counts[0]).astype(f32)
     valid_nodes = node_mask.astype(f32).reshape(slot_count, block_len) * live_slots[:, None]
@@ -471,8 +491,12 @@
         ],
         0,
     )
-    gathered = lax.all_gather(packed, both, axis=0, tiled=False)
-    low_ffn = lax.all_gather(ffn_weights.astype(bf16), both, axis=1, tiled=True)
+    gathered = doubled(packed, bits)
+    gathered, late_features = lax.optimization_barrier((gathered, features))
+    for index in (0, 1):
+        far_features[index] = passed_along(late_features, shifts[index])
+    far_features[2], late_ffn = lax.optimization_barrier((far_features[2], ffn_weights.astype(bf16)))
+    low_ffn = lax.all_gather(late_ffn, both, axis=1, tiled=True)
     low_proj = (
         gathered[:, : 5 * shard]
         .reshape(device_count, 5, shard, model_width)
@@ -544,9 +568,10 @@
     grad_hidden = nn(grad_ffn_y, low_ffn[1])
     grad_pre = gelu_back(grad_hidden)[0].astype(bf16)
     grad_up = tn(ffn_in, grad_pre)
-    shard_ffn = lax.psum_scatter(
-        jnp.stack([grad_up, grad_down]), both, scatter_dimension=1, tiled=True
-    )
+    order_x, order_y = orders_of(bits)
+    split = (device_count, shard, grad_up.shape[1])
+    shard_down = halved(grad_down.reshape(split), order_x)
+    shard_up = halved(grad_up.reshape(split), order_y)
     grad_ffn_in = nt(grad_pre, low_ffn[0])
     grad_mid_norm, grad_gain_two, grad_shift_two = norm_two_back(grad_ffn_in)
     grad_middle = grad_final + grad_mid_norm
@@ -554,29 +579,48 @@
     grad_out_proj = tn(attn_rows, grad_attn_y)
     grad_attn = nt(grad_attn_y, low_proj[4]).astype(bf16).reshape(query_blocks.shape)
 
-    grad_q, grad_own, grad_far, grad_bias = attend_back(
-        flat_nbr, pair_bias, query_blocks, grad_attn, lse, mask_cols, own_blocks, far_kv
-    )
+    head_of = (jnp.arange(model_width)[:, None] // HD == jnp.arange(H)[None, :]).astype(f32)
+    inner = lax.dot_general(
+        head_of,
+        grad_attn.reshape(row_count, model_width).astype(f32) * attn_rows.astype(f32),
+        (((0,), (1,)), ((), ())),
+        precision=precise,
+    )
+    inner = inner.reshape(H, slot_count, block_len).transpose(1, 0, 2).reshape(lse.shape)
+    low_kv = jnp.concatenate([low_proj[2], low_proj[3]], 1)
+    wide = (row_count, 2 * model_width)
+    pieces = [None] * 4
+    back = [None] * 4
+    part_q, far_ab, bias_ab = attend_back(
+        flat_nbr, pair_bias, query_blocks, grad_attn, lse, inner, mask_cols, None, None,
+        far_kv[2:], 4,
+    )
+    for index in (3, 2):
+        pieces[index] = far_ab[index - 2].reshape(wide)
+        ready = nt(pieces[index], low_kv).astype(bf16)
+        back[index] = passed_along(ready, -shifts[index])
+    grad_q, grad_own, near_ab, bias_near = attend_back(
+        flat_nbr, pair_bias, query_blocks, grad_attn, lse, inner, mask_cols, own_blocks, part_q,
+        far_kv[:2], 0,
+    )
+    for index in (0, 1):
+        pieces[index] = near_ab[index].reshape(wide)
+        ready = nt(pieces[index], low_kv).astype(bf16)
+        back[index] = passed_along(ready, -shifts[index])
+    grad_bias = jnp.concatenate([bias_near, bias_ab], 1)
     grad_q = grad_q.reshape(row_count, model_width)
-    grad_own = grad_own.reshape(row_count, 2 * model_width)
-    low_kv = jnp.concatenate([low_proj[2], low_proj[3]], 1)
-    back_pieces = []
-    for index, shift_by in reversed(list(enumerate(shifts))):
-        piece = grad_far[index].reshape(row_count, 2 * model_width)
-        back_pieces.append(passed_along(nt(piece, low_kv).astype(bf16), -shift_by))
+    grad_own = grad_own.reshape(wide)
     grad_query_w = tn(attn_in, grad_q)
     grad_kv_w = tn(attn_in, grad_own)
     for index in range(4):
-        grad_kv_w = grad_kv_w + tn(far_a1[index], grad_far[index].reshape(row_count, 2 * model_width))
-    early = jnp.stack(
-        [grad_query_w, grad_kv_w[:, :model_width], grad_kv_w[:, model_width:], grad_out_proj]
-    )
-    early = early.reshape(4, device_count, shard, model_width)
-    shard_early = [
-        halved(early[index], order) for index, order in enumerate(bit_orders(device_count))
-    ]
+        grad_kv_w = grad_kv_w + tn(far_a1[index], pieces[index])
+    split = (device_count, shard, model_width)
+    early_a = jnp.concatenate([grad_query_w.reshape(split), grad_out_proj.reshape(split)], 1)
+    early_b = grad_kv_w.reshape(device_count, shard, 2 * model_width)
+    early_a = halved(early_a, order_x)
+    early_b = halved(early_b, order_y)
     grad_attn_in = nt(grad_q, low_proj[1]) + nt(grad_own, low_kv)
-    for piece in back_pieces:
+    for piece in back:
         grad_attn_in = grad_attn_in + piece.astype(f32)
     _, norm_one_back = jax.vjp(layer_norm, base, gain_rows[0], gain_rows[1])
     grad_base_norm, grad_gain_one, grad_shift_one = norm_one_back(grad_attn_in)
@@ -584,30 +628,35 @@
     grad_encoder = tn(features, grad_base)
     bias_sums = jnp.sum(grad_bias.reshape(slot_count, listed + 1, H, block_len), -1)
     grad_table = jnp.einsum("sjt,sjh->th", type_onehot, bias_sums, precision=precise)
-    grad_vector_all = jnp.stack(
+    vector_rows = [
+        grad_gain_one,
+        grad_shift_one,
+        grad_gain_two,
+        grad_shift_two,
+        grad_gain_f,
+        grad_shift_f,
+        grad_head,
+        grad_table.reshape(model_width),
+    ]
+    which = jnp.arange(8)[:, None]
+    vector_sum = jnp.zeros((8, model_width), f32)
+    for index, row in enumerate(vector_rows):
+        vector_sum = jnp.where(which == index, row.reshape(1, model_width), vector_sum)
+    for bit in range(bits):
+        vector_sum = vector_sum + swap(vector_sum, bit)
+    place = lax.axis_index(both)
+    shard_vector = lax.dynamic_slice_in_dim(vector_sum, place * shard, shard, 1)
+    late = halved(grad_encoder.reshape(split), list(range(bits)))
+    shard_proj = jnp.stack(
         [
-            grad_gain_one,
-            grad_shift_one,
-            grad_gain_two,
-            grad_shift_two,
-            grad_gain_f,
-            grad_shift_f,
-            grad_head,
-            grad_table.reshape(model_width),
+            late,
+            early_a[:shard],
+            early_b[:, :model_width],
+            early_b[:, model_width:],
+            early_a[shard:],
         ]
     )
-    vector_lines = (
-        grad_vector_all.reshape(8, device_count, shard)
-        .transpose(1, 0, 2)
-        .reshape(device_count, 1, 8 * shard)
-    )
-    vector_lines = jnp.pad(vector_lines, ((0, 0), (0, 0), (0, model_width - 8 * shard)))
-    late = jnp.concatenate(
-        [grad_encoder.reshape(device_count, shard, model_width), vector_lines], 1
-    )
-    late = halved(late, list(range(device_count.bit_length() - 1)))
-    shard_proj = jnp.stack([late[:shard]] + shard_early)
-    shard_vector = late[shard, : 8 * shard].reshape(8, shard)
+    shard_ffn = jnp.stack([shard_up, shard_down])
 
     proj_parts = lamb_parts(proj_weights, shard_proj, proj_mean, proj_square, (1, 2))
     ffn_parts = lamb_parts(ffn_weights, shard_ffn, ffn_mean, ffn_square, (1, 2))
@@ -657,6 +706,7 @@
     cube = P(None, ("nodes", "fsdp"), None)
     flat = P(None, ("nodes", "fsdp"))
     state = (cube, cube, flat)
+
     return jax.shard_map(
         per_device,
         mesh=mesh,

time: 790 us -> 711 us (0.900)
  waiting for transfers between devices: 324 us -> 170 us
  starting transfers between devices: 85.1 us -> 165 us
  local copies, waits for them, and re-layouts: 76.7 us -> 63.4 us
  Pallas kernels: 135 us -> 145 us
    all_gather x2 -> x1, waiting for transfers between devices: 161 us -> 0.01 us  [per_device(): low_ffn = lax.all_gather(late_ffn, both, axis=1, tiled=True)]
    ppermute x8, waiting for transfers between devices: 0.02 us -> 73 us  [passed_along(): return lax.ppermute(value, 'nodes', pairs)]
    ppermute x25 -> x35, waiting for transfers between devices: 159 us -> 92.4 us  [swap(): return lax.ppermute(value, both, [(i, i ^ 1 << bit) for i in range(count)])]
    ppermute x8, starting transfers between devices: 9.84 us -> 51.7 us  [passed_along(): return lax.ppermute(value, 'nodes', pairs)]
    ppermute x25 -> x35, starting transfers between devices: 69.9 us -> 108 us  [swap(): return lax.ppermute(value, both, [(i, i ^ 1 << bit) for i in range(count)])]
    pallas_call x1 -> x2, Pallas kernels: 64.5 us -> 75.1 us  [attend_back(): pl.pallas_call(functools.partial(backward_body, listed, slots, bool(lead)...]
    another operation x10 -> x1, local copies, waits for them, and re-layouts: 8.2 us -> 0.01 us  [per_device(): jnp.stack([late, early_a[:shard], early_b[:, :model_width], early_b[:, mo...]
    unnamed x176 -> x213, local copies, waits for them, and re-layouts: 27.3 us -> 28 us
  transfers between devices with their start and end apart: 37 -> 45, of which waited for: 13 -> 27; matrix products, arithmetic and copies ran while one was open for 17% -> 12% of each run, Pallas kernels for 17% -> 10%
where the time goes in v2:
time: 711 us; the launch traced here: 703 us
  waiting for transfers between devices  170 us (24%)
  starting transfers between devices  165 us (23%)
  Pallas kernels  145 us (20%)
  matrix products  93.5 us (13%)
  local copies, waits for them, and re-layouts  63.4 us (9%)
  other arithmetic  46.1 us (6%)
  between operations  20 us (3%)
    ppermute x35, starting transfers between devices, swap(): return lax.ppermute(value, both, [(i, i ^ 1 << bit) for i in range(count)])  108 us
    ppermute x35, waiting for transfers between devices, swap(): return lax.ppermute(value, both, [(i, i ^ 1 << bit) for i in range(count)])  92.4 us
    pallas_call x2, Pallas kernels, attend_back(): pl.pallas_call(functools.partial(backward_body, listed, slots, bool(lead)...  75.1 us
    ppermute x8, waiting for transfers between devices, passed_along(): return lax.ppermute(value, 'nodes', pairs)  73 us
    ppermute x8, starting transfers between devices, passed_along(): return lax.ppermute(value, 'nodes', pairs)  51.7 us
    pallas_call x1, Pallas kernels, attend(): pl.pallas_call(functools.partial(forward_body, listed, slots), grid_spec=...  44.6 us
    dot_general x9, matrix products, nt(): lax.dot_general(a, b, (((1,), (1,)), ((), ())), preferred_element_type=f32)  33.5 us
    dot_general x3, matrix products, nn(): lax.dot_general(a, b, (((1,), (0,)), ((), ())), preferred_element_type=f32)  29.7 us
  transfers between devices with their start and end apart: 45, of which 27 were waited for; matrix products, arithmetic and copies ran while one was open for 12% of the time, Pallas kernels for 10%

profile of v2, /device:TPU:10, one launch (start us, length us, event | category | flops | bytes accessed | tf_op | source)
XLA Modules:
  0.0 703.1 jit_solution(11431566780474103908)
XLA Ops:
  17.5 34.5 %collective-permute-start.1 = (bf16[2,96,512]{2,1,0:T(8,128)(2,1)S(1)}, bf16[2,96,512]{2,1,0:T(8,128)(2,1)S(1)}, u32[]{:S(2)}, u32[]{:S(2)}) collective-permute-start(bf16[2,96,512]{2,1,0:T(8,128)(2,1)S(1)} %maximum_select_fusion.5), channel_id=1, source_target_pairs={{0,8},{1,9},{2,10},{3,11},{4,12},{5,13},{6,14},{7,15},{8,0},{9,1},... | collective-permute-start | bytes 589832 | tf_op jit(solution)/shard_map/ppermute | solution.py:413
  65.9 14.5 %collective-permute-done.3 = bf16[2,2,2,96,512]{4,3,2,1,0:T(8,128)(2,1)S(1)} collective-permute-done((bf16[2,2,2,96,512]{4,3,2,1,0:T(8,128)(2,1)}, bf16[2,2,2,96,512]{4,3,2,1,0:T(8,128)(2,1)S(1)}, u32[]{:S(2)}, u32[]{:S(2)}) %collective-permute-start.3) | collective-permute-done | bytes 786464 | tf_op jit(solution)/shard_map/ppermute | solution.py:413
  101.7 6.0 project_local.1
  130.6 22.2 %collective-permute-done.8.x_ref = bf16[1536,512]{1,0:T(8,128)(2,1)} collective-permute-done((bf16[1536,512]{1,0:T(8,128)(2,1)}, bf16[1536,512]{1,0:T(8,128)(2,1)}, u32[]{:S(2)}, u32[]{:S(2)}) %collective-permute-start.8) | collective-permute-done | bytes 1572896 | tf_op jit(solution)/shard_map/ppermute | solution.py:31
  168.1 5.5 project_remote.4
  173.7 44.6 %attention_forward.1 = (bf16[12,128,512]{2,1,0:T(8,128)(2,1)S(1)}, f32[12,1,1024]{2,1,0:T(1,128)S(1)}) custom-call(s32[96]{0:T(128)S(1)} %reshape.908.nbr_ref, f32[864]{0:T(1024)S(1)} %reshape.909.bias_ref, bf16[12,128,512]{2,1,0:T(8,128)(2,1)S(1)} %bitcast.312, f32[60,1,128]{2,1,0:T(1,128)S(1)} %add_multiply_fusion.1.mask_ref, ...), custom_call_target="tpu_custom_call" | custom-call | flops 7247757312 | bytes 28311552 | tf_op jit(solution)/shard_map/attention_forward/pallas_call | solution.py:225
  230.5 11.4 %multiply_convert_fusion = (bf16[1536,2048]{1,0:T(8,128)(2,1)S(1)}, f32[1536,2048]{1,0:T(8,128)}) fusion(bf16[2,512,2048]{2,1,0:T(8,128)(2,1)} %all-gather.2.cloned.1.call-done, f32[1536,512]{1,0:T(8,128)} %get-tuple-element.108, f32[512]{0:T(512)S(1)} %add.418, f32[512]{0:T(512)S(1)} %mul.532, f32[1536]{0:T(1024)S(1)} %fusion.50, ...), kind=kOutput, calls=%fused_computation.9 | convolution fusion | flops 3253469184 | bytes 24133632 | tf_op jit(solution)/shard_map/dot_general | solution.py:63
  241.9 5.6 fusion.70
  258.5 6.4 fusion.58
  264.9 13.1 %fusion.6 = bf16[1536,2048]{1,0:T(8,128)(2,1)S(1)} fusion(f32[1536,2048]{1,0:T(8,128)} %get-tuple-element.152, bf16[2,512,2048]{2,1,0:T(8,128)(2,1)S(1)} %copy-done.97, f32[1536]{0:T(1024)S(1)} %negate_multiply_fusion.2, f32[1536,512]{1,0:T(8,128)S(1)} %get-tuple-element.106, f32[1536]{0:T(1024)S(1)} %multiply_multiply_fusion.13, ...), kind=kOutput, calls=%fused_computation.8 | convolution fusion | flops 3291217920 | bytes 24162304 | tf_op jit(solution)/shard_map/dot_general | solution.py:63
  278.0 7.7 %fusion.60 = f32[512,2048]{1,0:T(8,128)} fusion(bf16[1536,2048]{1,0:T(8,128)(2,1)S(1)} %fusion.6, f32[1536,512]{1,0:T(8,128)} %get-tuple-element.108, f32[512]{0:T(512)S(1)} %add.418, f32[512]{0:T(512)S(1)} %mul.532, f32[1536]{0:T(1024)S(1)} %fusion.50, f32[1536]{0:T(1024)S(1)} %broadcast_multiply_fusion.2), kind=kOutput, calls=%fused_computation.256 | convolution fusion | flops 3225157632 | bytes 13647872 | tf_op jit(solution)/shard_map/dot_general | solution.py:71
  285.7 7.3 %multiply_reduce_fusion.2 = (f32[512]{0:T(512)S(1)}, f32[1536]{0:T(1024)S(1)}, f32[]{:T(128)}, f32[512]{0:T(512)S(1)}, f32[1536,512]{1,0:T(8,128)S(1)}) fusion(f32[1536,512]{1,0:T(8,128)} %get-tuple-element.108, f32[1536]{0:T(1024)S(1)} %fusion.50, f32[1536]{0:T(1024)S(1)} %broadcast_multiply_fusion.2, f32[512]{0:T(512)S(1)} %mul.532, ...), kind=kOutput, calls=%fused_computation.31 | convolution fusion | flops 3229873664 | bytes 14716932 | tf_op jit(solution)/shard_map/dot_general | solution.py:67
  305.3 35.4 %attention_backward_far.1 = (f32[12,128,512]{2,1,0:T(8,128)}, bf16[2,12,128,1024]{3,2,1,0:T(8,128)(2,1)}, f32[12,4,1024]{2,1,0:T(4,128)S(1)}) custom-call(s32[96]{0:T(128)S(1)} %reshape.908.nbr_ref, f32[864]{0:T(1024)S(1)} %reshape.909.bias_ref, bf16[12,128,512]{2,1,0:T(8,128)(2,1)S(1)} %bitcast.313, bf16[12,128,512]{2,1,0:T(8,128)(2,1)S(1)} %bitcast.295, ...), custom_call_target="tpu_custom_call" | custom-call | flops 16106127360 | bytes 12582912 | tf_op jit(solution)/shard_map/attention_backward_far/pallas_call | solution.py:379
  340.8 39.6 %attention_backward_near.1 = (bf16[12,128,512]{2,1,0:T(8,128)(2,1)S(1)}, bf16[12,128,1024]{2,1,0:T(8,128)(2,1)}, bf16[2,12,128,1024]{3,2,1,0:T(8,128)(2,1)}, f32[12,5,1024]{2,1,0:T(8,128)S(1)}) custom-call(s32[96]{0:T(128)S(1)} %reshape.908.nbr_ref, f32[864]{0:T(1024)S(1)} %reshape.909.bias_ref, bf16[12,128,512]{2,1,0:T(8,128)(2,1)S(1)} %bitcast.314, ...), custom_call_target="tpu_custom_call" | custom-call | flops 20132659200 | bytes 15728640 | tf_op jit(solution)/shard_map/attention_backward_near/pallas_call | solution.py:379
  387.4 40.1 %collective-permute-start.9 = (bf16[1536,512]{1,0:T(8,128)(2,1)}, bf16[1536,512]{1,0:T(8,128)(2,1)}, u32[]{:S(2)}, u32[]{:S(2)}) collective-permute-start(bf16[1536,512]{1,0:T(8,128)(2,1)} %convolution_convert_fusion.4), channel_id=1, source_target_pairs={{0,30},{2,0},{4,2},{6,4},{8,6},{10,8},{12,10},{14,12},{16,14},{18,... | collective-permute-start | bytes 4718600 | tf_op jit(solution)/shard_map/ppermute | solution.py:31
  476.6 18.6 %collective-permute-done.10 = bf16[1536,512]{1,0:T(8,128)(2,1)} collective-permute-done((bf16[1536,512]{1,0:T(8,128)(2,1)}, bf16[1536,512]{1,0:T(8,128)(2,1)}, u32[]{:S(2)}, u32[]{:S(2)}) %collective-permute-start.10) | collective-permute-done | bytes 1572896 | tf_op jit(solution)/shard_map/ppermute | solution.py:31
  495.3 12.8 %collective-permute-start.19 = (f32[2,2,2,32,512]{4,3,2,1,0:T(8,128)S(1)}, f32[2,2,2,32,512]{4,3,2,1,0:T(8,128)S(1)}, u32[]{:S(2)}, u32[]{:S(2)}) collective-permute-start(f32[2,2,2,32,512]{4,3,2,1,0:T(8,128)S(1)} %dynamic-slice_bitcast_fusion.5), channel_id=1, source_target_pairs={{0,2},{1,3},{2,0},{3,1},{4,6},{5,7},{6,4},{7,5},{8,10},{9,11},{10,... | collective-permute-start | bytes 1572872 | tf_op jit(solution)/shard_map/ppermute | solution.py:413
  508.1 32.2 %collective-permute-done.12 = bf16[1536,512]{1,0:T(8,128)(2,1)} collective-permute-done((bf16[1536,512]{1,0:T(8,128)(2,1)}, bf16[1536,512]{1,0:T(8,128)(2,1)}, u32[]{:S(2)}, u32[]{:S(2)}) %collective-permute-start.12) | collective-permute-done | bytes 1572896 | tf_op jit(solution)/shard_map/ppermute | solution.py:31
  540.4 5.3 multiply_reduce_fusion.1
  548.1 20.1 %collective-permute-start.20 = (f32[2,2,32,512]{3,2,1,0:T(8,128)S(1)}, f32[2,2,32,512]{3,2,1,0:T(8,128)S(1)}, u32[]{:S(2)}, u32[]{:S(2)}) collective-permute-start(f32[2,2,32,512]{3,2,1,0:T(8,128)S(1)} %dynamic-slice_bitcast_fusion.9), channel_id=1, source_target_pairs={{0,4},{1,5},{2,6},{3,7},{4,0},{5,1},{6,2},{7,3},{8,12},{9,13},{10,... | collective-permute-start | bytes 786440 | tf_op jit(solution)/shard_map/ppermute | solution.py:413
  603.8 6.7 collective-permute-done.14
  627.2 10.0 %collective-permute-done.29 = f32[2,2,2,16,2048]{4,3,2,1,0:T(8,128)S(1)} collective-permute-done((f32[2,2,2,16,2048]{4,3,2,1,0:T(8,128)S(1)}, f32[2,2,2,16,2048]{4,3,2,1,0:T(8,128)S(1)}, u32[]{:S(2)}, u32[]{:S(2)}) %collective-permute-start.29) | collective-permute-done | bytes 1048608 | tf_op jit(solution)/shard_map/ppermute | solution.py:413
  637.8 12.8 %collective-permute-done.34 = f32[2,2,2,16,2048]{4,3,2,1,0:T(8,128)S(1)} collective-permute-done((f32[2,2,2,16,2048]{4,3,2,1,0:T(8,128)S(1)}, f32[2,2,2,16,2048]{4,3,2,1,0:T(8,128)S(1)}, u32[]{:S(2)}, u32[]{:S(2)}) %collective-permute-start.34) | collective-permute-done | bytes 1048608 | tf_op jit(solution)/shard_map/ppermute | solution.py:413
  678.6 6.1 all-to-all-start
  (489 shorter events, 264.5 us)
Async XLA Ops:
  7.2 223.3 %all-gather.2.cloned.1.call-start = ((), (), s32[]{:S(2)}) async-start(), calls=%async_computation.1 | async-start | bytes 4325376 | tf_op jit(solution)/shard_map/all_gather | solution.py:499
  13.2 52.3 %collective-permute-start.7 = (bf16[1536,512]{1,0:T(8,128)(2,1)}, bf16[1536,512]{1,0:T(8,128)(2,1)S(1)}, u32[]{:S(2)}, u32[]{:S(2)}) collective-permute-start(bf16[1536,512]{1,0:T(8,128)(2,1)} %x_ref.1), channel_id=1, source_target_pairs={{0,8},{2,10},{4,12},{6,14},{8,16},{10,18},{12,20},{14,22},{16,24},... | collective-permute-start | bytes 4718600 | tf_op jit(solution)/shard_map/ppermute | solution.py:31
  17.5 38.2 %collective-permute-start.1 = (bf16[2,96,512]{2,1,0:T(8,128)(2,1)S(1)}, bf16[2,96,512]{2,1,0:T(8,128)(2,1)S(1)}, u32[]{:S(2)}, u32[]{:S(2)}) collective-permute-start(bf16[2,96,512]{2,1,0:T(8,128)(2,1)S(1)} %maximum_select_fusion.5), channel_id=1, source_target_pairs={{0,8},{1,9},{2,10},{3,11},{4,12},{5,13},{6,14},{7,15},{8,0},{9,1},... | collective-permute-start | bytes 589832 | tf_op jit(solution)/shard_map/ppermute | solution.py:413
  64.5 16.0 %collective-permute-start.3 = (bf16[2,2,2,96,512]{4,3,2,1,0:T(8,128)(2,1)}, bf16[2,2,2,96,512]{4,3,2,1,0:T(8,128)(2,1)S(1)}, u32[]{:S(2)}, u32[]{:S(2)}) collective-permute-start(bf16[2,2,2,96,512]{4,3,2,1,0:T(8,128)(2,1)} %maximum_select_fusion.2), channel_id=1, source_target_pairs={{0,2},{1,3},{2,0},{3,1},{4,6},{5,7},{6,4},{7,5},{8,10},{9,11},{10,... | collective-permute-start | bytes 2359304 | tf_op jit(solution)/shard_map/ppermute | solution.py:413
  81.8 70.9 %collective-permute-start.8 = (bf16[1536,512]{1,0:T(8,128)(2,1)}, bf16[1536,512]{1,0:T(8,128)(2,1)}, u32[]{:S(2)}, u32[]{:S(2)}) collective-permute-start(bf16[1536,512]{1,0:T(8,128)(2,1)} %x_ref.1), channel_id=1, source_target_pairs={{0,16},{2,18},{4,20},{6,22},{8,24},{10,26},{12,28},{14,30},{16,0},... | collective-permute-start | bytes 4718600 | tf_op jit(solution)/shard_map/ppermute | solution.py:31
  95.1 66.9 %collective-permute-start.6 = (bf16[1536,512]{1,0:T(8,128)(2,1)}, bf16[1536,512]{1,0:T(8,128)(2,1)}, u32[]{:S(2)}, u32[]{:S(2)}) collective-permute-start(bf16[1536,512]{1,0:T(8,128)(2,1)} %x_ref.1), channel_id=1, source_target_pairs={{0,30},{2,0},{4,2},{6,4},{8,6},{10,8},{12,10},{14,12},{16,14},{18,... | collective-permute-start | bytes 4718600 | tf_op jit(solution)/shard_map/ppermute | solution.py:31
  95.6 72.5 %collective-permute-start.5 = (bf16[1536,512]{1,0:T(8,128)(2,1)}, bf16[1536,512]{1,0:T(8,128)(2,1)}, u32[]{:S(2)}, u32[]{:S(2)}) collective-permute-start(bf16[1536,512]{1,0:T(8,128)(2,1)} %x_ref.1), channel_id=1, source_target_pairs={{0,2},{2,4},{4,6},{6,8},{8,10},{10,12},{12,14},{14,16},{16,18},{18... | collective-permute-start | bytes 4718600 | tf_op jit(solution)/shard_map/ppermute | solution.py:31
  387.4 89.1 %collective-permute-start.9 = (bf16[1536,512]{1,0:T(8,128)(2,1)}, bf16[1536,512]{1,0:T(8,128)(2,1)}, u32[]{:S(2)}, u32[]{:S(2)}) collective-permute-start(bf16[1536,512]{1,0:T(8,128)(2,1)} %convolution_convert_fusion.4), channel_id=1, source_target_pairs={{0,30},{2,0},{4,2},{6,4},{8,6},{10,8},{12,10},{14,12},{16,14},{18,... | collective-permute-start | bytes 4718600 | tf_op jit(solution)/shard_map/ppermute | solution.py:31
  430.5 64.7 %collective-permute-start.10 = (bf16[1536,512]{1,0:T(8,128)(2,1)}, bf16[1536,512]{1,0:T(8,128)(2,1)}, u32[]{:S(2)}, u32[]{:S(2)}) collective-permute-start(bf16[1536,512]{1,0:T(8,128)(2,1)} %convolution_convert_fusion.3), channel_id=1, source_target_pairs={{0,2},{2,4},{4,6},{6,8},{8,10},{10,12},{12,14},{14,16},{16,18},{18... | collective-permute-start | bytes 4718600 | tf_op jit(solution)/shard_map/ppermute | solution.py:31
  434.3 60.9 %collective-permute-start.11 = (bf16[1536,512]{1,0:T(8,128)(2,1)}, bf16[1536,512]{1,0:T(8,128)(2,1)}, u32[]{:S(2)}, u32[]{:S(2)}) collective-permute-start(bf16[1536,512]{1,0:T(8,128)(2,1)} %convolution_convert_fusion.2), channel_id=1, source_target_pairs={{0,24},{2,26},{4,28},{6,30},{8,0},{10,2},{12,4},{14,6},{16,8},{18,... | collective-permute-start | bytes 4718600 | tf_op jit(solution)/shard_map/ppermute | solution.py:31
  437.5 102.7 %collective-permute-start.12 = (bf16[1536,512]{1,0:T(8,128)(2,1)}, bf16[1536,512]{1,0:T(8,128)(2,1)}, u32[]{:S(2)}, u32[]{:S(2)}) collective-permute-start(bf16[1536,512]{1,0:T(8,128)(2,1)} %convolution_convert_fusion.1), channel_id=1, source_target_pairs={{0,16},{2,18},{4,20},{6,22},{8,24},{10,26},{12,28},{14,30},{16,0},... | collective-permute-start | bytes 4718600 | tf_op jit(solution)/shard_map/ppermute | solution.py:31
  452.2 11.5 %collective-permute-start.23 = (f32[2,2,2,2,16,1024]{5,4,3,1,0,2:T(8,128)S(1)}, f32[2,2,2,2,16,1024]{5,4,3,1,0,2:T(8,128)S(1)}, u32[]{:S(2)}, u32[]{:S(2)}) collective-permute-start(f32[2,2,2,2,16,1024]{5,4,3,1,0,2:T(8,128)S(1)} %bitcast.352), channel_id=1, source_target_pairs={{0,1},{1,0},{2,3},{3,2},{4,5},{5,4},{6,7},{7,6},{8,9},{9,8},{10,11... | collective-permute-start | bytes 3145736 | tf_op jit(solution)/shard_map/ppermute | solution.py:413
  473.9 129.6 %collective-permute-start.28 = (f32[2,2,2,2,16,2048]{5,4,3,1,0,2:T(8,128)S(1)}, f32[2,2,2,2,16,2048]{5,4,3,1,0,2:T(8,128)S(1)}, u32[]{:S(2)}, u32[]{:S(2)}) collective-permute-start(f32[2,2,2,2,16,2048]{5,4,3,1,0,2:T(8,128)S(1)} %bitcast.344), channel_id=1, source_target_pairs={{0,1},{1,0},{2,3},{3,2},{4,5},{5,4},{6,7},{7,6},{8,9},{9,8},{10,11... | collective-permute-start | bytes 6291464 | tf_op jit(solution)/shard_map/ppermute | solution.py:413
  476.5 143.2 %collective-permute-start.33 = (f32[2,2,2,2,16,2048]{5,4,2,1,0,3:T(8,128)S(1)}, f32[2,2,2,2,16,2048]{5,4,2,1,0,3:T(8,128)S(1)}, u32[]{:S(2)}, u32[]{:S(2)}) collective-permute-start(f32[2,2,2,2,16,2048]{5,4,2,1,0,3:T(8,128)S(1)} %bitcast.343), channel_id=1, source_target_pairs={{0,1},{1,0},{2,3},{3,2},{4,5},{5,4},{6,7},{7,6},{8,9},{9,8},{10,11... | collective-permute-start | bytes 6291464 | tf_op jit(solution)/shard_map/ppermute | solution.py:413
  495.2 50.8 %collective-permute-start.24 = (f32[2,2,2,16,1024]{4,3,2,1,0:T(8,128)S(1)}, f32[2,2,2,16,1024]{4,3,2,1,0:T(8,128)S(1)}, u32[]{:S(2)}, u32[]{:S(2)}) collective-permute-start(f32[2,2,2,16,1024]{4,3,2,1,0:T(8,128)S(1)} %dynamic-slice_bitcast_fusion.4), channel_id=1, source_target_pairs={{0,4},{1,5},{2,6},{3,7},{4,0},{5,1},{6,2},{7,3},{8,12},{9,13},{10,... | collective-permute-start | bytes 1572872 | tf_op jit(solution)/shard_map/ppermute | solution.py:413
  495.3 52.7 %collective-permute-start.19 = (f32[2,2,2,32,512]{4,3,2,1,0:T(8,128)S(1)}, f32[2,2,2,32,512]{4,3,2,1,0:T(8,128)S(1)}, u32[]{:S(2)}, u32[]{:S(2)}) collective-permute-start(f32[2,2,2,32,512]{4,3,2,1,0:T(8,128)S(1)} %dynamic-slice_bitcast_fusion.5), channel_id=1, source_target_pairs={{0,2},{1,3},{2,0},{3,1},{4,6},{5,7},{6,4},{7,5},{8,10},{9,11},{10,... | collective-permute-start | bytes 1572872 | tf_op jit(solution)/shard_map/ppermute | solution.py:413
  545.9 22.3 %collective-permute-start.38 = (f32[8,512]{1,0:T(8,128)S(1)}, f32[8,512]{1,0:T(8,128)S(1)}, u32[]{:S(2)}, u32[]{:S(2)}) collective-permute-start(f32[8,512]{1,0:T(8,128)S(1)} %select_select_fusion), channel_id=1, source_target_pairs={{0,1},{1,0},{2,3},{3,2},{4,5},{5,4},{6,7},{7,6},{8,9},{9,8},{10,11... | collective-permute-start | bytes 49160 | tf_op jit(solution)/shard_map/ppermute | solution.py:413
  546.1 41.9 %collective-permute-start.25 = (f32[2,2,16,1024]{3,2,1,0:T(8,128)S(1)}, f32[2,2,16,1024]{3,2,1,0:T(8,128)S(1)}, u32[]{:S(2)}, u32[]{:S(2)}) collective-permute-start(f32[2,2,16,1024]{3,2,1,0:T(8,128)S(1)} %dynamic-slice_bitcast_fusion.8), channel_id=1, source_target_pairs={{0,2},{1,3},{2,0},{3,1},{4,6},{5,7},{6,4},{7,5},{8,10},{9,11},{10,... | collective-permute-start | bytes 786440 | tf_op jit(solution)/shard_map/ppermute | solution.py:413
  548.1 41.2 %collective-permute-start.20 = (f32[2,2,32,512]{3,2,1,0:T(8,128)S(1)}, f32[2,2,32,512]{3,2,1,0:T(8,128)S(1)}, u32[]{:S(2)}, u32[]{:S(2)}) collective-permute-start(f32[2,2,32,512]{3,2,1,0:T(8,128)S(1)} %dynamic-slice_bitcast_fusion.9), channel_id=1, source_target_pairs={{0,4},{1,5},{2,6},{3,7},{4,0},{5,1},{6,2},{7,3},{8,12},{9,13},{10,... | collective-permute-start | bytes 786440 | tf_op jit(solution)/shard_map/ppermute | solution.py:413
  587.7 15.2 %collective-permute-start.13 = (f32[2,2,2,2,16,512]{5,4,2,1,0,3:T(8,128)S(1)}, f32[2,2,2,2,16,512]{5,4,2,1,0,3:T(8,128)S(1)}, u32[]{:S(2)}, u32[]{:S(2)}) collective-permute-start(f32[2,2,2,2,16,512]{5,4,2,1,0,3:T(8,128)S(1)} %bitcast.358), channel_id=1, source_target_pairs={{0,1},{1,0},{2,3},{3,2},{4,5},{5,4},{6,7},{7,6},{8,9},{9,8},{10,11... | collective-permute-start | bytes 1572872 | tf_op jit(solution)/shard_map/ppermute | solution.py:413
  612.7 24.5 %collective-permute-start.29 = (f32[2,2,2,16,2048]{4,3,2,1,0:T(8,128)S(1)}, f32[2,2,2,16,2048]{4,3,2,1,0:T(8,128)S(1)}, u32[]{:S(2)}, u32[]{:S(2)}) collective-permute-start(f32[2,2,2,16,2048]{4,3,2,1,0:T(8,128)S(1)} %dynamic-slice_bitcast_fusion.1), channel_id=1, source_target_pairs={{0,4},{1,5},{2,6},{3,7},{4,0},{5,1},{6,2},{7,3},{8,12},{9,13},{10,... | collective-permute-start | bytes 3145736 | tf_op jit(solution)/shard_map/ppermute | solution.py:413
  624.9 25.7 %collective-permute-start.34 = (f32[2,2,2,16,2048]{4,3,2,1,0:T(8,128)S(1)}, f32[2,2,2,16,2048]{4,3,2,1,0:T(8,128)S(1)}, u32[]{:S(2)}, u32[]{:S(2)}) collective-permute-start(f32[2,2,2,16,2048]{4,3,2,1,0:T(8,128)S(1)} %dynamic-slice_bitcast_fusion), channel_id=1, source_target_pairs={{0,2},{1,3},{2,0},{3,1},{4,6},{5,7},{6,4},{7,5},{8,10},{9,11},{10,... | collective-permute-start | bytes 3145736 | tf_op jit(solution)/shard_map/ppermute | solution.py:413
  637.4 18.8 %collective-permute-start.30 = (f32[2,2,16,2048]{3,2,1,0:T(8,128)S(1)}, f32[2,2,16,2048]{3,2,1,0:T(8,128)S(1)}, u32[]{:S(2)}, u32[]{:S(2)}) collective-permute-start(f32[2,2,16,2048]{3,2,1,0:T(8,128)S(1)} %dynamic-slice_bitcast_fusion.3), channel_id=1, source_target_pairs={{0,2},{1,3},{2,0},{3,1},{4,6},{5,7},{6,4},{7,5},{8,10},{9,11},{10,... | collective-permute-start | bytes 1572872 | tf_op jit(solution)/shard_map/ppermute | solution.py:413
  678.6 11.1 %all-to-all-start = ((f32[32,1,128]{2,1,0:T(1,128)}), f32[32,1,128]{2,1,0:T(1,128)S(1)}, u32[]{:S(2)}, u32[]{:S(2)}) async-start(f32[32,1,128]{2,1,0:T(1,128)} %broadcast_in_dim.170), calls=%async_computation | async-start | bytes 32768 | tf_op jit(solution)/shard_map/all_to_all | solution.py:672
  (123 other events, 1835.4 us)
Sparse Core Ops, SparseCore 0:
  65.7 151.1 all-gather.1
